TPU v7x, 256 devices: a whole 4x4x8 slice. The times are simulated.
256 devices in a mesh: seq: 64 (over y, z, core), head: 4 (over x).
Axes of the slice: x: 4, y: 4, z: 8, core: 2. Of those that a mesh axis runs over, the one named last changes fastest.
Arguments:
- queries: bfloat16 [32768, 3584], P(('seq', 'head')), may hold values from -256 to 256
- rotated_key_rows: bfloat16 [32768, 512], P(('seq', 'head')), may hold values from -5 to 5
- value_matrix: bfloat16 [32768, 512], P(('seq', 'head')), may hold values from -6 to 6
- cotangent: bfloat16 [32768, 3584], P(('seq', 'head')), may hold values from -6 to 6
- tree_mask: int32 [256, 4], P('seq'), may hold values from 0 to 1, as said below
Outputs:
- attention: bfloat16 [32768, 3584], P(('seq', 'head'))
- query_grad: bfloat16 [32768, 3584], P(('seq', 'head'))
- key_gradient: bfloat16 [32768, 512], P(('seq', 'head'))
- value_gradient: bfloat16 [32768, 512], P(('seq', 'head'))
Inputs may be any that keep to these rules, and one draw needn't show every extreme that they name: `tree_mask`: rows of the prompt's 4 blocks are 0. All blocks of one response share one row: 1 on its first r columns and 0 after, with r from 1 to 4; the first response reads all 4 prompt blocks.
All inputs are finite; a program needn't handle non-finite values.
Results may differ from a plain program's by a relative error of at most 0.034.
Values may be sent and summed in bfloat16 or wider, within the bound.
A program may use at most 128 MiB of HBM per device.

v0:
```python
import jax
import jax.numpy as jnp
from jax import lax
from jax.sharding import PartitionSpec as P

QUERY_HEADS = 28
KEY_VALUE_HEADS = 4
HEAD_SIZE = 128
MASK_BLOCK_SIZE = 128


def broadcast(value, axis, source):
    kept = jnp.where(lax.axis_index(axis) == source, value, 0).astype(value.dtype)
    return lax.psum(kept, axis)


def attend(query_head_count, block_keys, block_values, head_cotangents, allowed):
    score_scale = HEAD_SIZE ** (-0.5)
    scores = (
        jnp.einsum(
            "rjgd,njd->jgrn", query_head_count, block_keys, preferred_element_type=jnp.float32
        )
        * score_scale
    )
    scores = jnp.where(allowed, scores, jnp.float32(-1e30))
    row_max = jnp.max(scores, axis=-1, keepdims=True)
    weights = jnp.where(allowed, jnp.exp(scores - row_max), jnp.float32(0.0))
    softmax_probs = weights / jnp.sum(weights, axis=-1, keepdims=True)
    rounded_probs = softmax_probs.astype(jnp.bfloat16)
    attention = jnp.einsum(
        "jgrn,njd->rjgd", rounded_probs, block_values, preferred_element_type=jnp.float32
    ).astype(jnp.bfloat16)
    out_delta = jnp.sum(
        head_cotangents.astype(jnp.float32) * attention.astype(jnp.float32), axis=-1
    )
    out_delta = jnp.transpose(out_delta, (1, 2, 0))[..., None]
    dprob = jnp.einsum(
        "rjgd,njd->jgrn", head_cotangents, block_values, preferred_element_type=jnp.float32
    )
    dscore = (softmax_probs * (dprob - out_delta)).astype(jnp.bfloat16)
    query_grad = (
        jnp.einsum("jgrn,njd->rjgd", dscore, block_keys, preferred_element_type=jnp.float32)
        * score_scale
    ).astype(jnp.bfloat16)
    key_terms = (
        jnp.einsum("jgrn,rjgd->njd", dscore, query_head_count, preferred_element_type=jnp.float32)
        * score_scale
    )
    value_terms = jnp.einsum(
        "jgrn,rjgd->njd", rounded_probs, head_cotangents, preferred_element_type=jnp.float32
    )
    return (attention, query_grad, key_terms, value_terms)


def on_device(queries, rotated_key_rows, value_matrix, cotangent, tree_mask):
    seq_index = lax.axis_index("seq")
    key_local, value_local = (
        lax.all_gather(rotated_key_rows, "head", axis=0, tiled=True),
        lax.all_gather(value_matrix, "head", axis=0, tiled=True),
    )
    start_row = lax.axis_index("head") * queries.shape[0]
    row_count = queries.shape[0]
    seg_tokens = key_local.shape[0]
    kv_local = key_local.shape[1] // HEAD_SIZE
    group_width = QUERY_HEADS // KEY_VALUE_HEADS
    prompt_keys, prompt_values = (broadcast(key_local, "seq", 0), broadcast(value_local, "seq", 0))
    block_keys = jnp.concatenate([prompt_keys, key_local], 0).reshape(
        2 * seg_tokens, kv_local, HEAD_SIZE
    )
    block_values = jnp.concatenate([prompt_values, value_local], 0).reshape(
        2 * seg_tokens, kv_local, HEAD_SIZE
    )
    token_mask = jnp.repeat(jnp.repeat(tree_mask, MASK_BLOCK_SIZE, axis=0), MASK_BLOCK_SIZE, axis=1)
    mask_rows = lax.dynamic_slice_in_dim(token_mask, start_row, row_count, 0)
    prompt_reads = (mask_rows > 0) & (seq_index > 0)
    positions = start_row + jnp.arange(row_count, dtype=jnp.int32)
    causal = jnp.arange(seg_tokens, dtype=jnp.int32)[None, :] <= positions[:, None]
    allowed = jnp.concatenate([prompt_reads, causal], 1)
    query_head_count = queries.reshape(row_count, kv_local, group_width, HEAD_SIZE)
    head_cotangents = cotangent.reshape(row_count, kv_local, group_width, HEAD_SIZE)
    attention, query_grad, key_terms, value_terms = attend(
        query_head_count, block_keys, block_values, head_cotangents, allowed
    )
    attention = attention.reshape(row_count, kv_local * group_width * HEAD_SIZE)
    query_grad = query_grad.reshape(row_count, kv_local * group_width * HEAD_SIZE)
    prompt_key_terms = key_terms[:seg_tokens].reshape(seg_tokens, kv_local * HEAD_SIZE)
    prompt_value_terms = value_terms[:seg_tokens].reshape(seg_tokens, kv_local * HEAD_SIZE)
    own_key = key_terms[seg_tokens:].reshape(seg_tokens, kv_local * HEAD_SIZE)
    own_value = value_terms[seg_tokens:].reshape(seg_tokens, kv_local * HEAD_SIZE)
    is_owner = seq_index == 0
    summed_key, summed_value, share_key, share_value = (
        lax.psum_scatter(own_key, "head", scatter_dimension=0, tiled=True),
        lax.psum_scatter(own_value, "head", scatter_dimension=0, tiled=True),
        lax.psum_scatter(prompt_key_terms, "head", scatter_dimension=0, tiled=True),
        lax.psum_scatter(prompt_value_terms, "head", scatter_dimension=0, tiled=True),
    )
    owner_key, owner_value = lax.psum((share_key, share_value), "seq")
    key_gradient = (summed_key + jnp.where(is_owner, owner_key, jnp.float32(0.0))).astype(
        jnp.bfloat16
    )
    value_gradient = (summed_value + jnp.where(is_owner, owner_value, jnp.float32(0.0))).astype(
        jnp.bfloat16
    )
    return (attention, query_grad, key_gradient, value_gradient)


def solution(mesh):
    in_specs = (
        P(("seq", "head"), None),
        P(("seq", "head"), None),
        P(("seq", "head"), None),
        P(("seq", "head"), None),
        P("seq", None),
    )
    out_specs = (
        P(("seq", "head"), None),
        P(("seq", "head"), None),
        P(("seq", "head"), None),
        P(("seq", "head"), None),
    )
    return jax.shard_map(
        on_device, mesh=mesh, in_specs=in_specs, out_specs=out_specs, check_vma=False
    )
```

profile of v0, /device:TPU:2, one launch (start us, length us, event | category | flops | bytes accessed | tf_op | source)
XLA Modules:
  0.0 558.8 jit_solution(60528525411168746)
XLA Ops:
  7.2 0.0 copy-start.6
  7.2 0.0 all-reduce.7.cloned.1.call-start
  7.2 1.1 copy.29
  8.3 1.0 copy.27
  9.4 15.0 %all_gather.6 = bf16[512,512]{0,1:T(8,128)(2,1)S(1)} all-gather(bf16[128,512]{0,1:T(8,128)(2,1)S(1)} %copy.27), channel_id=1, replica_groups=mesh['seq'=64,'head'=4] {'head'}, dimensions={0}, use_global_device_ids=true | all-gather | bytes 655360 | tf_op jit(solution)/shard_map/all_gather | solution.py:59
  24.3 13.2 %all_gather.7 = bf16[512,512]{0,1:T(8,128)(2,1)S(1)} all-gather(bf16[128,512]{0,1:T(8,128)(2,1)S(1)} %copy.29), channel_id=1, replica_groups=mesh['seq'=64,'head'=4] {'head'}, dimensions={0}, use_global_device_ids=true | all-gather | bytes 655360 | tf_op jit(solution)/shard_map/all_gather | solution.py:58
  37.5 0.8 broadcast_select_fusion
  38.4 0.8 broadcast_select_fusion.1
  39.2 0.0 all-reduce.7.cloned.1.call-update
  39.2 0.0 reduce-scatter.11.cloned.1.call-start
  39.3 0.8 copy.28
  40.1 0.1 broadcast_bitcast_fusion
  40.1 2.2 copy.30
  42.4 0.0 copy-done.6
  42.4 0.6 copy.34
  43.0 0.1 broadcast_in_dim.35
  43.1 0.1 iota_compare_fusion
  43.2 183.0 %all-reduce.7.cloned.1.call-done = (bf16[512,512]{0,1:T(8,128)(2,1)}, bf16[512,512]{0,1:T(8,128)(2,1)}) async-done(((bf16[512,512]{0,1:T(8,128)(2,1)}, bf16[512,512]{0,1:T(8,128)(2,1)}), (bf16[512,512]{0,1:T(8,128)(2,1)}, bf16[512,512]{0,1:T(8,128)(2,1)})) %all-reduce.7.cloned.1.call-update) | async-done | bytes 1048592 | tf_op jit(solution)/shard_map/psum | solution.py:14
  226.3 2.5 pad_maximum_fusion
  228.8 10.1 %fusion.16 = (f32[4,7,128]{2,1,0:T(8,128)S(1)}, f32[4,7,128,1024]{2,3,1,0:T(8,128)}) fusion(pred[128,1024]{0,1:T(8,128)(4,1)S(1)} %pad_add_fusion, bf16[1024,4,128,1]{0,2,3,1:T(8,128)(2,1)S(1)} %bitcast.84, bf16[128,4,7,128]{0,3,2,1:T(8,128)(2,1)} %bitcast.93), kind=kOutput, calls=%fused_computation.36 | convolution fusion | flops 957875200 | bytes 16791552 | tf_op jit(solution)/shard_map/sub | solution.py:27
  238.9 9.9 %fusion.7 = bf16[4,7,128,1024]{2,3,1,0:T(8,128)(2,1)} fusion(f32[4,7,128,1024]{2,3,1,0:T(8,128)} %get-tuple-element.21, f32[4,7,128]{2,1,0:T(8,128)S(1)} %get-tuple-element.20), kind=kLoop, calls=%fused_computation.11 | loop fusion | flops 7340032 | bytes 22034432 | tf_op jit(solution)/shard_map/convert_element_type | solution.py:29
  248.7 0.0 copy-start
  248.7 0.0 copy-start.2
  248.7 5.7 %convolution_bitcast_fusion = f32[1024,4,128]{0,2,1:T(8,128)S(1)} fusion(bf16[4,7,128,1024]{2,3,1,0:T(8,128)(2,1)} %fusion.7, bf16[128,4,7,128]{0,3,2,1:T(8,128)(2,1)S(1)} %bitcast.81), kind=kOutput, calls=%fused_computation.16 | convolution fusion | flops 939524096 | bytes 10354688 | tf_op jit(solution)/shard_map/jgrn,rjgd->njd/dot_general | solution.py:49
  254.4 0.0 copy-done
  254.4 0.0 copy-done.2
  254.4 2.3 multiply_reduce_fusion
  256.7 1.5 fusion.14
  258.2 2.5 copy.43
  260.7 0.0 reduce-scatter.11.cloned.1.call-update
  260.8 0.2 reduce-scatter.7.cloned.1.call-start
  261.0 0.0 copy-start.5
  261.0 6.6 %fusion.2 = bf16[4,7,128,1024]{2,3,1,0:T(8,128)(2,1)S(1)} fusion(bf16[1024,4,128,1]{0,2,3,1:T(8,128)(2,1)S(1)} %bitcast.87, bf16[128,4,7,128]{0,3,2,1:T(8,128)(2,1)S(1)} %bitcast.83, f32[4,7,128]{2,1,0:T(8,128)S(1)} %bitcast.98, f32[4,7,128,1024]{2,3,1,0:T(8,128)} %get-tuple-element.21, f32[4,7,128]{2,1,0:T(8,128)S(1)} %get-tuple-element.20), kind=kOutput, calls=%fused_computation.3 | convolution fusion | flops 954204160 | bytes 24014848 | tf_op jit(solution)/shard_map/rjgd,njd->jgrn/dot_general | solution.py:37
  267.6 0.0 copy-start.1
  267.6 2.9 copy-done.1
  270.6 0.0 copy-done.5
  270.6 0.0 copy-start.3
  270.6 2.5 fusion.8
  273.0 1.2 fusion.15
  274.2 2.6 copy.40
  276.9 0.0 reduce-scatter.7.cloned.1.call-update
  276.9 0.0 reduce-scatter.9.cloned.1.call-start
  276.9 0.0 copy-done.3
  277.0 1.3 copy.42
  278.3 0.0 reduce-scatter.9.cloned.1.call-update
  278.3 0.0 all-reduce.5.cloned.1.call-start
  278.4 4.3 reduce-scatter.11.cloned.1.call-done
  282.7 28.4 %reduce-scatter.7.cloned.1.call-done = f32[128,512]{1,0:T(8,128)} async-done(((f32[512,512]{1,0:T(8,128)}), f32[128,512]{1,0:T(8,128)}) %reduce-scatter.7.cloned.1.call-update) | async-done | bytes 262160 | tf_op jit(solution)/shard_map/reduce_scatter | solution.py:94
  311.1 0.0 copy-start.4
  311.1 0.0 all-reduce.5.cloned.1.call-update
  311.1 0.0 reduce-scatter.5.cloned.1.call-start
  311.2 1.4 copy.39
  312.6 0.0 reduce-scatter.5.cloned.1.call-update
  312.6 4.4 multiply_convert_fusion
  317.0 1.3 copy.45
  318.3 0.0 copy-done.4
  318.3 1.3 copy.44
  319.5 20.0 %reduce-scatter.9.cloned.1.call-done = f32[128,512]{1,0:T(8,128)} async-done(((f32[512,512]{1,0:T(8,128)}), f32[128,512]{1,0:T(8,128)}) %reduce-scatter.9.cloned.1.call-update) | async-done | bytes 262160 | tf_op jit(solution)/shard_map/reduce_scatter | solution.py:93
  339.5 186.5 %all-reduce.5.cloned.1.call-done = (f32[128,512]{1,0:T(8,128)}, f32[128,512]{1,0:T(8,128)}) async-done(((f32[128,512]{1,0:T(8,128)}, f32[128,512]{1,0:T(8,128)}), (f32[128,512]{1,0:T(8,128)}, f32[128,512]{1,0:T(8,128)})) %all-reduce.5.cloned.1.call-update) | async-done | bytes 524304 | tf_op jit(solution)/shard_map/psum | solution.py:97
  526.0 1.7 add_convert_fusion
  527.8 22.5 %reduce-scatter.5.cloned.1.call-done = f32[128,512]{1,0:T(8,128)} async-done(((f32[512,512]{1,0:T(8,128)}), f32[128,512]{1,0:T(8,128)}) %reduce-scatter.5.cloned.1.call-update) | async-done | bytes 262160 | tf_op jit(solution)/shard_map/reduce_scatter | solution.py:92
  550.2 1.7 add_convert_fusion.1
  (3 shorter events, 0.0 us)
Async XLA Ops:
  7.2 35.2 %copy-start.6 = (bf16[128,3584]{1,0:T(8,128)(2,1)S(1)}, bf16[128,3584]{1,0:T(8,128)(2,1)}, u32[]{:S(2)}) copy-start(bf16[128,3584]{1,0:T(8,128)(2,1)} %param.8) | copy-start | bytes 2752516
  7.2 219.1 %all-reduce.7.cloned.1.call-start = ((), (), s32[]{:S(2)}) async-start(), calls=%async_computation.9 | async-start | bytes 2097152 | tf_op jit(solution)/shard_map/psum | solution.py:14
  39.2 243.4 %reduce-scatter.11.cloned.1.call-start = ((), (), s32[]{:S(2)}) async-start(), calls=%async_computation.7 | async-start | bytes 1310720 | tf_op jit(solution)/shard_map/reduce_scatter | solution.py:95
  248.7 5.7 %copy-start = (bf16[4,7,128,1024]{2,3,1,0:T(8,128)(2,1)S(1)}, bf16[4,7,128,1024]{2,3,1,0:T(8,128)(2,1)}, u32[]{:S(2)}) copy-start(bf16[4,7,128,1024]{2,3,1,0:T(8,128)(2,1)} %fusion.7) | copy-start | bytes 22020100
  248.7 5.7 %copy-start.2 = (bf16[1024,512]{0,1:T(8,128)(2,1)S(1)}, bf16[1024,512]{0,1:T(8,128)(2,1)}, u32[]{:S(2)}) copy-start(bf16[1024,512]{0,1:T(8,128)(2,1)} %get-tuple-element.24) | copy-start | bytes 3145732
  260.8 50.4 %reduce-scatter.7.cloned.1.call-start = ((), (), s32[]{:S(2)}) async-start(), calls=%async_computation.5 | async-start | bytes 1310720 | tf_op jit(solution)/shard_map/reduce_scatter | solution.py:94
  261.0 9.6 %copy-start.5 = (bf16[128,3584]{0,1:T(8,128)(2,1)S(1)}, bf16[128,3584]{0,1:T(8,128)(2,1)}, u32[]{:S(2)}) copy-start(bf16[128,3584]{0,1:T(8,128)(2,1)} %copy.30) | copy-start | bytes 2752516
  267.6 2.9 copy-start.1
  270.6 6.4 %copy-start.3 = (f32[512,4,128]{0,2,1:T(8,128)S(1)}, f32[512,4,128]{0,2,1:T(8,128)}, u32[]{:S(2)}) copy-start(f32[512,4,128]{0,2,1:T(8,128)} %get-tuple-element.16) | copy-start | bytes 3145732
  276.9 62.6 %reduce-scatter.9.cloned.1.call-start = ((), (), s32[]{:S(2)}) async-start(), calls=%async_computation.6 | async-start | bytes 1310720 | tf_op jit(solution)/shard_map/reduce_scatter | solution.py:93
  278.3 247.7 %all-reduce.5.cloned.1.call-start = ((), (), s32[]{:S(2)}) async-start(), calls=%async_computation.8 | async-start | bytes 1048576 | tf_op jit(solution)/shard_map/psum | solution.py:97
  311.1 7.1 %copy-start.4 = (bf16[4,128,7,128]{3,1,2,0:T(8,128)(2,1)S(1)}, bf16[4,128,7,128]{3,1,2,0:T(8,128)(2,1)}, u32[]{:S(2)}) copy-start(bf16[4,128,7,128]{3,1,2,0:T(8,128)(2,1)} %get-tuple-element.23) | copy-start | bytes 2752516
  311.1 239.1 %reduce-scatter.5.cloned.1.call-start = ((), (), s32[]{:S(2)}) async-start(), calls=%async_computation.4 | async-start | bytes 1310720 | tf_op jit(solution)/shard_map/reduce_scatter | solution.py:92
Sparse Core Ops, SparseCore 0:
  39.4 186.8 all-reduce.6
  260.9 21.7 reduce-scatter.10
  285.2 25.8 reduce-scatter.6
  313.7 25.8 reduce-scatter.8
  342.9 183.0 all-reduce.4
  528.4 21.7 reduce-scatter.4
where the time goes:
time: 561 us; the launch traced here: 559 us
  waiting for transfers between devices  445 us (79%)
  matrix products  31.4 us (6%)
  blocking collectives  28.2 us (5%)
  local copies, waits for them, and re-layouts  22 us (4%)
  other arithmetic  17.6 us (3%)
  between operations  14.3 us (3%)
    psum x1, waiting for transfers between devices, on_device(): owner_key, owner_value = lax.psum((share_key, share_value), 'seq')  186 us
    psum x1, waiting for transfers between devices, broadcast(): return lax.psum(kept, axis)  183 us
    reduce_scatter x1, waiting for transfers between devices, on_device(): lax.psum_scatter(prompt_key_terms, 'head', scatter_dimension=0, tiled=True)  28.4 us
    reduce_scatter x1, waiting for transfers between devices, on_device(): lax.psum_scatter(own_key, 'head', scatter_dimension=0, tiled=True)  22.5 us
    reduce_scatter x1, waiting for transfers between devices, on_device(): lax.psum_scatter(own_value, 'head', scatter_dimension=0, tiled=True)  20 us
    all_gather x1, blocking collectives, on_device(): lax.all_gather(value_matrix, 'head', axis=0, tiled=True)  15 us
    all_gather x1, blocking collectives, on_device(): lax.all_gather(rotated_key_rows, 'head', axis=0, tiled=True)  13.2 us
    unnamed x23, local copies, waits for them, and re-layouts  11.3 us
  transfers between devices with their start and end apart: 6, of which 6 were waited for; matrix products, arithmetic and copies ran while one was open for 5% of the time, Pallas kernels for 0%

commit v1 on v0

v1 whole, which is shorter than its diff:
```python
import jax
import jax.numpy as jnp
from jax import lax
from jax.experimental import pallas as pl
from jax.experimental.pallas import tpu as pltpu
from jax.sharding import PartitionSpec as P

HEADS = 4
GROUP = 7
D = 128
QUARTERS = 4
NY, NZ = 4, 8
SCALE = D ** (-0.5)
LOG2E = 1.4426950408889634
MESH = pl.DeviceIdType.MESH
BF16 = jnp.bfloat16
F32 = jnp.float32


def place():
    seq = lax.axis_index("seq")
    x = lax.axis_index("head")
    return x, seq // (2 * NZ), (seq // 2) % NZ, seq % 2


def device(x, y, z, core):
    return ((y * NZ + z) * 2 + core, x)


def remote(src, dst, send_sem, recv_sem, target):
    return pltpu.make_async_remote_copy(
        src_ref=src,
        dst_ref=dst,
        send_sem=send_sem,
        recv_sem=recv_sem,
        device_id=target,
        device_id_type=MESH,
    )


def partners(x, j):
    flip, mirror = x + 1 - 2 * (x % 2), 3 - x
    return (flip, mirror) if j % 2 == 0 else (mirror, flip)


def signal(sem, targets):
    for target in targets:
        pl.semaphore_signal(sem, inc=1, device_id=target, device_id_type=MESH)


def greet(x, y, z, core, tree):
    sem = pltpu.get_barrier_semaphore()
    column, leaf, top = tree & (z == 0), tree & (z != 0), tree & (z == 0) & (y == 0)
    child = tree & (z == 0) & (y != 0)

    @pl.when(top)
    def _():
        signal(sem, [device(x, n, 0, core) for n in (2, 1, 3)])

    @pl.when(column)
    def _():
        signal(sem, [device(x, y, n, core) for n in (4, 3, 5, 2, 6, 1, 7)])

    @pl.when(child)
    def _():
        signal(sem, [device(x, 0, 0, core)])

    @pl.when(leaf)
    def _():
        signal(sem, [device(x, y, 0, core)])

    pa, pb = partners(x, 0)
    signal(sem, [device(pa, y, z, core), device(pb, y, z, core), device(x, y, z, 1 - core)])
    for role, peers in ((top, 2 + NZ + NY - 1), (child, 2 + NZ + 1), (leaf, 4), (~(column | leaf), 3)):
        @pl.when(role)
        def _():
            pl.semaphore_wait(sem, peers)


def gather_kernel(k_ref, v_ref, kv_ref, lsem, s_own, r_own, s_pr, r_pr, s_y, s_z, r_t, s_c, r_c):
    x, y, z, core = place()
    opp = (x + 2) % 4
    is_c0, is_c1 = core == 0, core == 1
    is_root = (core == 0) & (z == 0) & (y == 0)
    column = (core == 0) & (z == 0)
    leaf = (core == 0) & (z != 0)

    def local(j, block, base):
        return [
            pltpu.make_async_copy(
                ref.at[:, pl.ds(j * D, D)], kv_ref.at[j, block, t], lsem.at[base, j, t]
            )
            for t, ref in enumerate((k_ref, v_ref))
        ]

    for j in range(HEADS):
        for copy in local(j, 4 + x, 0):
            copy.start()

    @pl.when(is_root)
    def _():
        for j in range(HEADS):
            for copy in local(j, x, 1):
                copy.start()

    greet(x, y, z, core, core == 0)

    def y_send(j, n):
        blk = kv_ref.at[j, x]
        return remote(blk, blk, s_y.at[j, n - 1], r_t.at[j], device(x, n, 0, 0))

    def z_send(j, n):
        blk = kv_ref.at[j, x]
        return remote(blk, blk, s_z.at[j, n - 1], r_t.at[j], device(x, y, n, 0))

    def x_sends(j, base, ss, rs):
        pa, pb = partners(x, j)
        own, first = kv_ref.at[j, base + x], kv_ref.at[j, base + pa]
        to_a, to_b = device(pa, y, z, core), device(pb, y, z, core)
        return (
            remote(own, own, ss.at[j, 0], rs.at[j, 0], to_a),
            remote(own, own, ss.at[j, 1], rs.at[j, 1], to_b),
            remote(first, first, ss.at[j, 2], rs.at[j, 2], to_b),
        )

    def x_arrival(j, base, ss, rs, i):
        pa, pb = partners(x, j)
        blk = kv_ref.at[j, base + (pa, pb, opp)[i]]
        remote(blk, blk, ss.at[j, i], rs.at[j, i], device((pa, pb, pb)[i], y, z, core)).wait_recv()

    def core_send(j):
        blk = kv_ref.at[j, pl.ds(0, 4)]
        return remote(blk, blk, s_c.at[j], r_c.at[j], device(x, y, z, 1 - core))

    @pl.when(is_root)
    def _():
        for j in range(HEADS):
            for copy in local(j, x, 1):
                copy.wait()
            for n in (2, 1, 3):
                y_send(j, n).start()

    for j in range(HEADS):
        for copy in local(j, 4 + x, 0):
            copy.wait()
        sends = x_sends(j, 4, s_own, r_own)
        sends[0].start()
        sends[1].start()

    @pl.when(is_c0)
    def _():
        for j in range(HEADS):
            @pl.when(column & (y != 0))
            def _():
                y_send(j, y).wait_recv()

            @pl.when(column)
            def _():
                for n in (4, 5, 3, 6, 2, 7, 1):
                    z_send(j, n).start()

            @pl.when(leaf)
            def _():
                z_send(j, z).wait_recv()

            sends = x_sends(j, 0, s_pr, r_pr)
            sends[0].start()
            sends[1].start()
            x_arrival(j, 4, s_own, r_own, 0)
            x_sends(j, 4, s_own, r_own)[2].start()
        for j in range(HEADS):
            x_arrival(j, 0, s_pr, r_pr, 0)
            x_sends(j, 0, s_pr, r_pr)[2].start()
        for j in range(HEADS):
            x_arrival(j, 0, s_pr, r_pr, 1)
            x_arrival(j, 0, s_pr, r_pr, 2)
            core_send(j).start()
        for j in range(HEADS):
            for copy in x_sends(j, 0, s_pr, r_pr):
                copy.wait_send()
            core_send(j).wait_send()

    @pl.when(is_c1)
    def _():
        for j in range(HEADS):
            x_arrival(j, 4, s_own, r_own, 0)
            x_sends(j, 4, s_own, r_own)[2].start()
        for j in range(HEADS):
            core_send(j).wait_recv()

    for j in range(HEADS):
        x_arrival(j, 4, s_own, r_own, 1)
        x_arrival(j, 4, s_own, r_own, 2)
        for copy in x_sends(j, 4, s_own, r_own):
            copy.wait_send()

    @pl.when(column)
    def _():
        for j in range(HEADS):
            for n in range(1, NZ):
                z_send(j, n).wait_send()

    @pl.when(is_root)
    def _():
        for j in range(HEADS):
            for n in range(1, NY):
                y_send(j, n).wait_send()


def gather(k, v):
    dma = pltpu.SemaphoreType.DMA
    return pl.pallas_call(
        gather_kernel,
        out_shape=jax.ShapeDtypeStruct((HEADS, 8, 2, D, D), BF16),
        in_specs=[pl.BlockSpec(memory_space=pltpu.VMEM)] * 2,
        out_specs=pl.BlockSpec(memory_space=pltpu.VMEM),
        scratch_shapes=[
            dma((2, HEADS, 2)),
            dma((HEADS, 3)),
            dma((HEADS, 3)),
            dma((HEADS, 3)),
            dma((HEADS, 3)),
            dma((HEADS, NY - 1)),
            dma((HEADS, NZ - 1)),
            dma((HEADS,)),
            dma((HEADS,)),
            dma((HEADS,)),
        ],
        compiler_params=pltpu.CompilerParams(collective_id=0, has_side_effects=True),
        name="gather_keys_values",
    )(k, v)


def nt(a, b):
    return lax.dot_general(a, b, (((1,), (1,)), ((), ())), preferred_element_type=F32)


def nn(a, b):
    return lax.dot_general(a, b, (((1,), (0,)), ((), ())), preferred_element_type=F32)


def attend_kernel(mask_ref, q_ref, c_ref, kv_ref, att_ref, dq_ref, g_ref, bias, ps, dss, qs, cs):
    x = lax.axis_index("head")
    seq = lax.axis_index("seq")

    @pl.when(pl.program_id(0) == 0)
    def _():
        key = lax.broadcasted_iota(jnp.int32, (D, D), 0)
        query = lax.broadcasted_iota(jnp.int32, (D, D), 1)
        for b in range(QUARTERS):
            reads = jnp.where(seq > 0, mask_ref[x, b], 0)
            level = jnp.where(reads > 0, 0.0, -1e30).astype(F32)
            bias[pl.ds(b * D, D), :] = jnp.full((D, D), level, F32)
            seen = key + b * D <= query + x * D
            bias[pl.ds((4 + b) * D, D), :] = jnp.where(seen, 0.0, -1e30).astype(F32)

    keys = kv_ref[0, :, 0].reshape(8 * D, D)
    values = kv_ref[0, :, 1].reshape(8 * D, D)
    keys_t, values_t = keys.T, values.T
    for h in range(GROUP):
        cols = pl.ds(h * D, D)
        q, c = q_ref[:, cols], c_ref[:, cols]
        qs[cols, :] = q
        cs[cols, :] = c
        s = nt(keys, q) + bias[...]
        top = jnp.max(s, axis=0, keepdims=True)
        p = jnp.exp2((s - top) * (SCALE * LOG2E))
        p = p * (1.0 / jnp.sum(p, axis=0, keepdims=True))
        rounded = p.astype(BF16)
        ps[:, cols] = rounded
        out_t = nn(values_t, rounded)
        att = out_t.T.astype(BF16)
        att_ref[:, cols] = att
        delta = jnp.sum(c.astype(F32).T * out_t.astype(BF16).astype(F32), axis=0, keepdims=True)
        ds = (p * (nt(values, c) - delta)).astype(BF16)
        dss[:, cols] = ds
        dq_ref[:, cols] = (nn(keys_t, ds) * SCALE).T.astype(BF16)
    g_ref[0, :, 0] = (nn(dss[...], qs[...]) * SCALE).reshape(8, D, D)
    g_ref[0, :, 1] = nn(ps[...], cs[...]).reshape(8, D, D)


def attend(mask, q, c, kv):
    wide = pl.BlockSpec((D, GROUP * D), lambda j: (0, j))
    cubes = pl.BlockSpec((1, 8, 2, D, D), lambda j: (j, 0, 0, 0, 0))
    return pl.pallas_call(
        attend_kernel,
        grid=(HEADS,),
        out_shape=(
            jax.ShapeDtypeStruct(q.shape, BF16),
            jax.ShapeDtypeStruct(q.shape, BF16),
            jax.ShapeDtypeStruct((HEADS, 8, 2, D, D), F32),
        ),
        in_specs=[pl.BlockSpec(memory_space=pltpu.SMEM), wide, wide, cubes],
        out_specs=(wide, wide, cubes),
        scratch_shapes=[
            pltpu.VMEM((8 * D, D), F32),
            pltpu.VMEM((8 * D, GROUP * D), BF16),
            pltpu.VMEM((8 * D, GROUP * D), BF16),
            pltpu.VMEM((GROUP * D, D), BF16),
            pltpu.VMEM((GROUP * D, D), BF16),
        ],
        compiler_params=pltpu.CompilerParams(dimension_semantics=("arbitrary",)),
        name="attend",
    )(mask, q, c, kv)


def reduce_kernel(
    g_ref, dk_ref, dv_ref,
    so1, ro1, so2, ro2, sc, rc, gs, sp1, rp1, sp2, rp2, part, sz, rz, sy, ry, rv,
    ss, rs, s_y, r_y, s_z, r_z, s_v, r_v,
):
    x, y, z, core = place()
    opp = (x + 2) % 4
    is_root = (core == 0) & (z == 0) & (y == 0)
    root_pair = (core == 1) & (z == 0) & (y == 0)

    greet(x, y, z, core, z >= 0)

    def own1(j):
        return remote(so1.at[j], ro1.at[j], ss.at[0, j], rs.at[0, j], device(partners(x, j)[0], y, z, core))

    def own2(j):
        return remote(so2.at[j], ro2.at[j], ss.at[1, j], rs.at[1, j], device(partners(x, j)[1], y, z, core))

    def pair(j):
        return remote(sc.at[j], rc.at[j], ss.at[2, j], rs.at[2, j], device(x, y, z, 1 - core))

    def pr1(j):
        return remote(sp1.at[j], rp1.at[j], ss.at[3, j], rs.at[3, j], device(partners(x, j)[0], y, z, core))

    def pr2(j):
        return remote(sp2.at[j], rp2.at[j], ss.at[4, j], rs.at[4, j], device(partners(x, j)[1], y, z, core))

    def to_column(j, n):
        return remote(sz.at[j], rz.at[j, n - 1], s_z.at[j], r_z.at[j, n - 1], device(x, y, 0, core))

    def to_root(j, n):
        return remote(sy.at[j], ry.at[j, n - 1], s_y.at[j], r_y.at[j, n - 1], device(x, 0, 0, core))

    def hand_over(j):
        return remote(part.at[j], rv.at[j], s_v.at[j], r_v.at[j], device(x, y, z, 1 - core))

    for j in range(HEADS):
        for q in range(QUARTERS):
            sc[j, q] = g_ref[j, q, 1 - core].astype(BF16)
        pair(j).start()
    for j in range(HEADS):
        pa, pb = partners(x, j)
        so1[j, 0] = g_ref[j, 4 + pa].astype(BF16)
        so1[j, 1] = g_ref[j, 4 + opp].astype(BF16)
        own1(j).start()
    for j in range(HEADS):
        pa, pb = partners(x, j)
        pair(j).wait_recv()
        for q in range(QUARTERS):
            gs[j, q] = g_ref[j, q, core] + rc[j, q].astype(F32)
        sp1[j, 0] = gs[j, pa].astype(BF16)
        sp1[j, 1] = gs[j, opp].astype(BF16)
        pr1(j).start()
    for j in range(HEADS):
        pa, pb = partners(x, j)
        pr1(j).wait_recv()
        sp2[j] = (gs[j, pb] + rp1[j, 1].astype(F32)).astype(BF16)
        pr2(j).start()
    for j in range(HEADS):
        pa, pb = partners(x, j)
        own1(j).wait_recv()
        so2[j] = (g_ref[j, 4 + pb] + ro1[j, 1].astype(F32)).astype(BF16)
        own2(j).start()
    for j in range(HEADS):
        pr2(j).wait_recv()
        total = gs[j, x] + rp1[j, 0].astype(F32) + rp2[j].astype(F32)
        part[j] = total
        sz[j] = total.astype(BF16)

        @pl.when(z != 0)
        def _():
            to_column(j, z).start()

    @pl.when(z == 0)
    def _():
        for j in range(HEADS):
            total = part[j]
            for n in range(1, NZ):
                to_column(j, n).wait_recv()
                total = total + rz[j, n - 1].astype(F32)
            part[j] = total
            sy[j] = total.astype(BF16)

            @pl.when(y != 0)
            def _():
                to_root(j, y).start()

    @pl.when((z == 0) & (y == 0))
    def _():
        for j in range(HEADS):
            total = part[j]
            for n in range(1, NY):
                to_root(j, n).wait_recv()
                total = total + ry[j, n - 1].astype(F32)
            part[j] = total

            @pl.when(core == 1)
            def _():
                hand_over(j).start()

    for j in range(HEADS):
        own2(j).wait_recv()
        cols = pl.ds(j * D, D)
        total = g_ref[j, 4 + x] + ro1[j, 0].astype(F32) + ro2[j].astype(F32)
        dk_ref[:, cols] = total[0].astype(BF16)
        dv_ref[:, cols] = total[1].astype(BF16)

    @pl.when(is_root)
    def _():
        for j in range(HEADS):
            hand_over(j).wait_recv()
            cols = pl.ds(j * D, D)
            total = g_ref[j, 4 + x] + ro1[j, 0].astype(F32) + ro2[j].astype(F32)
            dk_ref[:, cols] = (total[0] + part[j]).astype(BF16)
            dv_ref[:, cols] = (total[1] + rv[j]).astype(BF16)

    for j in range(HEADS):
        for copy in (own1(j), own2(j), pair(j), pr1(j), pr2(j)):
            copy.wait_send()

        @pl.when(z != 0)
        def _():
            to_column(j, z).wait_send()

        @pl.when((z == 0) & (y != 0))
        def _():
            to_root(j, y).wait_send()

        @pl.when(root_pair)
        def _():
            hand_over(j).wait_send()


def reduce(g):
    dma = pltpu.SemaphoreType.DMA
    block = (D, D)
    vmem = pltpu.VMEM
    out = jax.ShapeDtypeStruct((D, HEADS * D), BF16)
    return pl.pallas_call(
        reduce_kernel,
        out_shape=(out, out),
        in_specs=[pl.BlockSpec(memory_space=pltpu.VMEM)],
        out_specs=(pl.BlockSpec(memory_space=pltpu.VMEM),) * 2,
        scratch_shapes=[
            vmem((HEADS, 2, 2) + block, BF16),
            vmem((HEADS, 2, 2) + block, BF16),
            vmem((HEADS, 2) + block, BF16),
            vmem((HEADS, 2) + block, BF16),
            vmem((HEADS, 4) + block, BF16),
            vmem((HEADS, 4) + block, BF16),
            vmem((HEADS, 4) + block, F32),
            vmem((HEADS, 2) + block, BF16),
            vmem((HEADS, 2) + block, BF16),
            vmem((HEADS,) + block, BF16),
            vmem((HEADS,) + block, BF16),
            vmem((HEADS,) + block, F32),
            vmem((HEADS,) + block, BF16),
            vmem((HEADS, NZ - 1) + block, BF16),
            vmem((HEADS,) + block, BF16),
            vmem((HEADS, NY - 1) + block, BF16),
            vmem((HEADS,) + block, F32),
            dma((5, HEADS)),
            dma((5, HEADS)),
            dma((HEADS,)),
            dma((HEADS, NY - 1)),
            dma((HEADS,)),
            dma((HEADS, NZ - 1)),
            dma((HEADS,)),
            dma((HEADS,)),
        ],
        compiler_params=pltpu.CompilerParams(collective_id=1, has_side_effects=True),
        name="reduce_gradients",
    )(g)


def on_device(queries, rotated_key_rows, value_matrix, cotangent, tree_mask):
    kv = gather(rotated_key_rows, value_matrix)
    attention, query_grad, terms = attend(tree_mask, queries, cotangent, kv)
    key_gradient, value_gradient = reduce(terms)
    return (attention, query_grad, key_gradient, value_gradient)


def solution(mesh):
    rows = P(("seq", "head"), None)
    return jax.shard_map(
        on_device,
        mesh=mesh,
        in_specs=(rows, rows, rows, rows, P("seq", None)),
        out_specs=(rows, rows, rows, rows),
        check_vma=False,
    )
```

time: 561 us -> 101 us (0.18)
  waiting for transfers between devices: 445 us -> 0 us
  Pallas kernels: 0 us -> 95.3 us
  matrix products: 31.4 us -> 0 us
  blocking collectives: 28.2 us -> 0 us
  local copies, waits for them, and re-layouts: 22 us -> 3.14 us
  other arithmetic: 17.6 us -> 0 us
  between operations: 14.3 us -> 0.65 us
    psum x2 -> x0, waiting for transfers between devices: 370 us -> none  [the longest x1 186 us: on_device(): owner_key, owner_value = lax.psum((share_key, share_value), 'seq')]
    pallas_call x0 -> x3, Pallas kernels: none -> 95.3 us  [the longest x1 44.1 us: reduce(): pl.pallas_call(reduce_kernel, out_shape=(out, out), in_specs=[pl.BlockSpe...]
    reduce_scatter x4 -> x0, waiting for transfers between devices: 75.2 us -> none  [the longest x1 28.4 us: on_device(): lax.psum_scatter(prompt_key_terms, 'head', scatter_dimension=0, tiled=True)]
    all_gather x2 -> x0, blocking collectives: 28.2 us -> none  [the longest x1 15 us: on_device(): lax.all_gather(value_matrix, 'head', axis=0, tiled=True)]
    dot_general x5 -> x0, matrix products: 21.4 us -> none  [the longest x1 6.61 us: attend(): jnp.einsum('rjgd,njd->jgrn', head_cotangents, block_values, preferred_ele...]
    convert_element_type x3 -> x0, other arithmetic: 13.3 us -> none  [the longest x1 9.85 us: attend(): rounded_probs = softmax_probs.astype(jnp.bfloat16)]
    sub x1 -> x0, matrix products: 10.1 us -> none  [attend(): weights = jnp.where(allowed, jnp.exp(scores - row_max), jnp.float32(0.0))]
    unnamed x23 -> x2, local copies, waits for them, and re-layouts: 11.3 us -> 3.14 us
  transfers between devices with their start and end apart: 6 -> 0, of which waited for: 6 -> 0; matrix products, arithmetic and copies ran while one was open for 5% -> 0% of each run, Pallas kernels for 0% -> 0%
where the time goes in v1:
time: 101 us; the launch traced here: 99.1 us
  Pallas kernels  95.3 us (94%)
  local copies, waits for them, and re-layouts  3.14 us (3%)
    pallas_call x1, Pallas kernels, reduce(): pl.pallas_call(reduce_kernel, out_shape=(out, out), in_specs=[pl.BlockSpe...  44.1 us
    pallas_call x1, Pallas kernels, gather(): pl.pallas_call(gather_kernel, out_shape=jax.ShapeDtypeStruct((HEADS, 8, 2...  26.1 us
    pallas_call x1, Pallas kernels, attend(): pl.pallas_call(attend_kernel, grid=(HEADS,), out_shape=(jax.ShapeDtypeStr...  25 us
    unnamed x2, local copies, waits for them, and re-layouts  3.14 us

profile of v1, /device:TPU:2, one launch (start us, length us, event | category | flops | bytes accessed | tf_op | source)
XLA Modules:
  0.0 99.1 jit_solution(7554127487795598209)
XLA Ops:
  0.6 26.1 %gather_keys_values.1.kv_ref = bf16[4,8,2,128,128]{4,3,2,1,0:T(8,128)(2,1)} custom-call(bf16[128,512]{1,0:T(8,128)(2,1)} %k_ref.1, bf16[128,512]{1,0:T(8,128)(2,1)} %v_ref.1), custom_call_target="tpu_custom_call" | custom-call | tf_op jit(solution)/shard_map/gather_keys_values/pallas_call | solution.py:212
  26.8 25.0 %attend.1 = (bf16[128,3584]{1,0:T(8,128)(2,1)}, bf16[128,3584]{1,0:T(8,128)(2,1)}, f32[4,8,2,128,128]{4,3,2,1,0:T(8,128)}) custom-call(s32[4,4]{1,0:T(4,128)} %mask_ref.1, bf16[128,3584]{1,0:T(8,128)(2,1)} %q_ref.1, bf16[128,3584]{1,0:T(8,128)(2,1)} %c_ref.1, bf16[4,8,2,128,128]{4,3,2,1,0:T(8,128)(2,1)} %gather_keys_values.1.kv_ref), custom_call_target="tpu_custom_call" | custom-call | tf_op jit(solution)/shard_map/attend/pallas_call | solution.py:285
  51.8 44.1 %reduce_gradients.1 = (bf16[128,512]{1,0:T(8,128)(2,1)}, bf16[128,512]{1,0:T(8,128)(2,1)}) custom-call(f32[4,8,2,128,128]{4,3,2,1,0:T(8,128)} %get-tuple-element.11.g_ref), custom_call_target="tpu_custom_call" | custom-call | tf_op jit(solution)/shard_map/reduce_gradients/pallas_call | solution.py:445
  95.9 1.6 %copy.11 = bf16[128,512]{1,0:T(8,128)(2,1)} copy(bf16[128,512]{1,0:T(8,128)(2,1)} %get-tuple-element.20) | data formatting | bytes 262144
  97.5 1.6 %copy.12 = bf16[128,512]{1,0:T(8,128)(2,1)} copy(bf16[128,512]{1,0:T(8,128)(2,1)} %get-tuple-element.21) | data formatting | bytes 262144

commit v2 on v1

v2 whole, which is shorter than its diff:
```python
import jax
import jax.numpy as jnp
from jax import lax
from jax.experimental import pallas as pl
from jax.experimental.pallas import tpu as pltpu
from jax.sharding import PartitionSpec as P

HEADS = 4
GROUP = 7
D = 128
QUARTERS = 4
NY, NZ = 4, 8
SCALE = D ** (-0.5)
LOG2E = 1.4426950408889634
MESH = pl.DeviceIdType.MESH
BF16 = jnp.bfloat16
F32 = jnp.float32


def place():
    seq = lax.axis_index("seq")
    x = lax.axis_index("head")
    return x, seq // (2 * NZ), (seq // 2) % NZ, seq % 2


def device(x, y, z, core):
    return ((y * NZ + z) * 2 + core, x)


def remote(src, dst, send_sem, recv_sem, target):
    return pltpu.make_async_remote_copy(
        src_ref=src,
        dst_ref=dst,
        send_sem=send_sem,
        recv_sem=recv_sem,
        device_id=target,
        device_id_type=MESH,
    )


def partners(x, j):
    flip, mirror = x + 1 - 2 * (x % 2), 3 - x
    return (flip, mirror) if j % 2 == 0 else (mirror, flip)


def signal(sem, targets):
    for target in targets:
        pl.semaphore_signal(sem, inc=1, device_id=target, device_id_type=MESH)


def greet(x, y, z, core, tree):
    sem = pltpu.get_barrier_semaphore()
    column, leaf, top = tree & (z == 0), tree & (z != 0), tree & (z == 0) & (y == 0)
    child = tree & (z == 0) & (y != 0)

    @pl.when(top)
    def _():
        signal(sem, [device(x, n, 0, core) for n in (2, 1, 3)])

    @pl.when(column)
    def _():
        signal(sem, [device(x, y, n, core) for n in (4, 3, 5, 2, 6, 1, 7)])

    @pl.when(child)
    def _():
        signal(sem, [device(x, 0, 0, core)])

    @pl.when(leaf)
    def _():
        signal(sem, [device(x, y, 0, core)])

    pa, pb = partners(x, 0)
    signal(sem, [device(pa, y, z, core), device(pb, y, z, core), device(x, y, z, 1 - core)])
    for role, peers in ((top, 2 + NZ + NY - 1), (child, 2 + NZ + 1), (leaf, 4), (~(column | leaf), 3)):
        @pl.when(role)
        def _():
            pl.semaphore_wait(sem, peers)


TILES = ((0, 256), (256, 256), (512, 256), (768, 128))
WIDE = GROUP * D
EXP_SCALE = SCALE * LOG2E


def nt(a, b):
    return lax.dot_general(a, b, (((1,), (1,)), ((), ())), preferred_element_type=F32)


def nn(a, b):
    return lax.dot_general(a, b, (((1,), (0,)), ((), ())), preferred_element_type=F32)


def fold_max(a):
    return jnp.max(a.reshape(D // 8, 8, a.shape[1]), axis=0)


def fold_sum(a):
    return jnp.sum(a.reshape(D // 8, 8, a.shape[1]), axis=0)


def main_kernel(
    mask_ref, k_ref, v_ref, q_hbm, c_hbm,
    att_hbm, dq_hbm, dk_ref, dv_ref,
    kv, q_s, c_s, att_s, dq_s, bias, po, dpo, mo, lo, sp, dpp, ps, dss, vt,
    g, so1, ro1, so2, ro2, sc, rc, gs, sp1, rp1, sp2, rp2, part, sz, rz, sy, ry, rv,
    lsem, qsem, osem, s_own, r_own, s_pr, r_pr, s_by, s_bz, r_t, s_c, r_c,
    ss, rs, s_y, r_y, s_z, r_z, s_v, r_v,
):
    x, y, z, core = place()
    opp = (x + 2) % 4
    seq = lax.axis_index("seq")
    top_row = (z == 0) & (y == 0)
    is_root = top_row & (core == 0)
    root_pair = top_row & (core == 1)
    column = (core == 0) & (z == 0)
    leaf = (core == 0) & (z != 0)

    def local(j, block, base):
        return [
            pltpu.make_async_copy(ref.at[:, pl.ds(j * D, D)], kv.at[j, block, t], lsem.at[base, j, t])
            for t, ref in enumerate((k_ref, v_ref))
        ]

    for j in range(HEADS):
        for copy in local(j, 4 + x, 0):
            copy.start()

    @pl.when(is_root)
    def _():
        for j in range(HEADS):
            for copy in local(j, x, 1):
                copy.start()

    for j in range(HEADS):
        for h in range(GROUP):
            cols, rows = pl.ds((j * GROUP + h) * D, D), pl.ds(h * D, D)
            pltpu.make_async_copy(q_hbm.at[:, cols], q_s.at[j, rows], qsem.at[0, j]).start()
            pltpu.make_async_copy(c_hbm.at[:, cols], c_s.at[j, rows], qsem.at[1, j]).start()

    def take_out(buf, hbm, i, j):
        for h in range(GROUP):
            cols, rows = pl.ds((j * GROUP + h) * D, D), pl.ds(h * D, D)
            pltpu.make_async_copy(buf.at[j, rows], hbm.at[:, cols], osem.at[i, j]).start()

    greet(x, y, z, core, z >= 0)

    def y_send(j, n):
        blk = kv.at[j, x]
        return remote(blk, blk, s_by.at[j, n - 1], r_t.at[j], device(x, n, 0, 0))

    def z_send(j, n):
        blk = kv.at[j, x]
        return remote(blk, blk, s_bz.at[j, n - 1], r_t.at[j], device(x, y, n, 0))

    def x_send(j, base, ss, rs, i):
        pa, pb = partners(x, j)
        blk = kv.at[j, base + (x, x, pa)[i]]
        return remote(blk, blk, ss.at[j, i], rs.at[j, i], device((pa, pb, pb)[i], y, z, core))

    def x_arrival(j, base, ss, rs, i):
        pa, pb = partners(x, j)
        blk = kv.at[j, base + (pa, pb, opp)[i]]
        remote(blk, blk, ss.at[j, i], rs.at[j, i], device((pa, pb, pb)[i], y, z, core)).wait_recv()

    def core_send(j):
        blk = kv.at[j, pl.ds(0, 4)]
        return remote(blk, blk, s_c.at[j], r_c.at[j], device(x, y, z, 1 - core))

    @pl.when(is_root)
    def _():
        for j in range(HEADS):
            for copy in local(j, x, 1):
                copy.wait()
            for n in (2, 1, 3):
                y_send(j, n).start()

    for j in range(HEADS):
        for copy in local(j, 4 + x, 0):
            copy.wait()
        x_send(j, 4, s_own, r_own, 0).start()
        x_send(j, 4, s_own, r_own, 1).start()

    key = lax.broadcasted_iota(jnp.int32, (D, D), 0)
    query = lax.broadcasted_iota(jnp.int32, (D, D), 1)
    for b in range(QUARTERS):
        seen = key + b * D <= query + x * D
        tile = jnp.where(seen, 0.0, -1e30).astype(F32)
        bias[pl.ds(b * D, D), pl.ds(0, D)] = tile
        bias[pl.ds(b * D, D), pl.ds(D, D)] = tile
    levels = []
    for b in range(QUARTERS):
        reads = jnp.where(seq > 0, mask_ref[x, b], 0)
        levels.append(jnp.where(reads > 0, 0.0, -1e30).astype(F32))

    def relay(j):
        @pl.when(column)
        def _():
            @pl.when(y != 0)
            def _():
                y_send(j, y).wait_recv()

            for n in (4, 5, 3, 6, 2, 7, 1):
                z_send(j, n).start()

        x_arrival(j, 4, s_own, r_own, 0)
        x_send(j, 4, s_own, r_own, 2).start()

    def prompt1(j):
        @pl.when(core == 0)
        def _():
            @pl.when(leaf)
            def _():
                z_send(j, z).wait_recv()

            x_send(j, 0, s_pr, r_pr, 0).start()
            x_send(j, 0, s_pr, r_pr, 1).start()

    def prompt2(j):
        @pl.when(core == 0)
        def _():
            x_arrival(j, 0, s_pr, r_pr, 0)
            x_send(j, 0, s_pr, r_pr, 2).start()

    def prompt3(j):
        @pl.when(core == 0)
        def _():
            x_arrival(j, 0, s_pr, r_pr, 1)
            x_arrival(j, 0, s_pr, r_pr, 2)
            core_send(j).start()

    def prompt_here(j):
        @pl.when(core == 1)
        def _():
            core_send(j).wait_recv()

    def own_part(j):
        x_arrival(j, 4, s_own, r_own, 1)
        x_arrival(j, 4, s_own, r_own, 2)
        pltpu.make_async_copy(q_s.at[j], q_s.at[j], qsem.at[0, j]).wait()
        pltpu.make_async_copy(c_s.at[j], c_s.at[j], qsem.at[1, j]).wait()
        for at, width in TILES:
            cols = pl.ds(at, width)
            keys = kv[j, 4:8, 0].reshape(4 * D, D)
            values = kv[j, 4:8, 1].reshape(4 * D, D)
            po[j, :, cols] = nt(keys, q_s[j, cols, :]) + bias[:, pl.ds(0, width)]
            top = None
            for b in range(QUARTERS):
                part_top = fold_max(po[j, pl.ds(b * D, D), cols])
                top = part_top if top is None else jnp.maximum(top, part_top)
            top = jnp.max(top, axis=0, keepdims=True)
            total = None
            for b in range(QUARTERS):
                p = jnp.exp2((po[j, pl.ds(b * D, D), cols] - top) * EXP_SCALE)
                po[j, pl.ds(b * D, D), cols] = p
                part_sum = fold_sum(p)
                total = part_sum if total is None else total + part_sum
            mo[j, :, cols] = top
            lo[j, :, cols] = jnp.sum(total, axis=0, keepdims=True)
            dpo[j, :, cols] = nt(values, c_s[j, cols, :])

    def flip_values(j):
        for b in range(2 * QUARTERS):
            vt[:, pl.ds(b * D, D)] = kv[j, b, 1].T

    def prompt_part(j, at, width):
        cols, wide = pl.ds(at, width), pl.ds(0, width)
        c = c_s[j, cols, :]
        sp[:, wide] = nt(kv[j, 0:4, 0].reshape(4 * D, D), q_s[j, cols, :])
        dpp[:, wide] = nt(kv[j, 0:4, 1].reshape(4 * D, D), c)
        own_top = mo[j, :, cols]
        top = None
        for b in range(QUARTERS):
            part_top = fold_max(sp[pl.ds(b * D, D), wide]) + levels[b]
            top = part_top if top is None else jnp.maximum(top, part_top)
        top = jnp.maximum(own_top, jnp.max(top, axis=0, keepdims=True))
        shrink = jnp.exp2((own_top - top) * EXP_SCALE)
        total = None
        for b in range(QUARTERS):
            rows = pl.ds(b * D, D)
            p = jnp.exp2((sp[rows, wide] - (top - levels[b])) * EXP_SCALE)
            sp[rows, wide] = p
            part_sum = fold_sum(p)
            total = part_sum if total is None else total + part_sum
        total = jnp.sum(total, axis=0, keepdims=True) + lo[j, :, cols] * shrink
        inverse = 1.0 / total
        shrink = shrink * inverse
        for b in range(QUARTERS):
            rows = pl.ds(b * D, D)
            ps[rows, cols] = (sp[rows, wide] * inverse).astype(BF16)
            ps[pl.ds((4 + b) * D, D), cols] = (po[j, rows, cols] * shrink).astype(BF16)
        out_t = nn(vt[...], ps[:, cols]).astype(BF16)
        deltas = []
        for i in range(width // D):
            lanes, rows = slice(i * D, i * D + D), pl.ds(at + i * D, D)
            att_s[j, rows, :] = out_t[:, lanes].T
            prod = c_s[j, rows, :].T.astype(F32) * out_t[:, lanes].astype(F32)
            deltas.append(jnp.sum(prod, axis=0, keepdims=True))
        delta = jnp.concatenate(deltas, axis=1)
        for b in range(QUARTERS):
            rows = pl.ds(b * D, D)
            dss[j, rows, cols] = ((sp[rows, wide] * inverse) * (dpp[rows, wide] - delta)).astype(BF16)
            dss[j, pl.ds((4 + b) * D, D), cols] = (
                (po[j, rows, cols] * shrink) * (dpo[j, rows, cols] - delta)
            ).astype(BF16)

    def key_terms(j, first):
        rows = pl.ds(first * D, 4 * D)
        g[j, first : first + 4, 0] = (nn(dss[j, rows, :], q_s[j]) * SCALE).reshape(4, D, D)
        g[j, first : first + 4, 1] = nn(ps[rows, :], c_s[j]).reshape(4, D, D)

    def query_part(j):
        for b in range(2 * QUARTERS):
            vt[:, pl.ds(b * D, D)] = kv[j, b, 0].T
        for at, width in TILES:
            grad_t = (nn(vt[...], dss[j, :, pl.ds(at, width)]) * SCALE).astype(BF16)
            for i in range(width // D):
                dq_s[j, pl.ds(at + i * D, D), :] = grad_t[:, i * D : i * D + D].T
        take_out(dq_s, dq_hbm, 1, j)

    def hop(send, arrive, i, j, target):
        return remote(send.at[j], arrive.at[j], ss.at[i, j], rs.at[i, j], target)

    def own1(j):
        return hop(so1, ro1, 0, j, device(partners(x, j)[0], y, z, core))

    def own2(j):
        return hop(so2, ro2, 1, j, device(partners(x, j)[1], y, z, core))

    def pair(j):
        return hop(sc, rc, 2, j, device(x, y, z, 1 - core))

    def pr1(j):
        return hop(sp1, rp1, 3, j, device(partners(x, j)[0], y, z, core))

    def pr2(j):
        return hop(sp2, rp2, 4, j, device(partners(x, j)[1], y, z, core))

    def to_column(j, n):
        return remote(sz.at[j], rz.at[j, n - 1], s_z.at[j], r_z.at[j, n - 1], device(x, y, 0, core))

    def to_root(j, n):
        return remote(sy.at[j], ry.at[j, n - 1], s_y.at[j], r_y.at[j, n - 1], device(x, 0, 0, core))

    def hand_over(j):
        return remote(part.at[j], rv.at[j], s_v.at[j], r_v.at[j], device(x, y, z, 1 - core))

    def reduce0(j):
        for b in range(QUARTERS):
            sc[j, b] = g[j, b, 1 - core].astype(BF16)
        pair(j).start()

    def own_reduce1(j):
        pa, pb = partners(x, j)
        so1[j, 0] = g[j, 4 + pa].astype(BF16)
        so1[j, 1] = g[j, 4 + opp].astype(BF16)
        own1(j).start()

    def reduce1(j):
        pa, pb = partners(x, j)
        pair(j).wait_recv()
        for b in range(QUARTERS):
            gs[j, b] = g[j, b, core] + rc[j, b].astype(F32)
        sp1[j, 0] = gs[j, pa].astype(BF16)
        sp1[j, 1] = gs[j, opp].astype(BF16)
        pr1(j).start()

    def reduce2(j):
        pa, pb = partners(x, j)
        pr1(j).wait_recv()
        sp2[j] = (gs[j, pb] + rp1[j, 1].astype(F32)).astype(BF16)
        pr2(j).start()

    def own_reduce2(j):
        pa, pb = partners(x, j)
        own1(j).wait_recv()
        so2[j] = (g[j, 4 + pb] + ro1[j, 1].astype(F32)).astype(BF16)
        own2(j).start()

    def reduce3(j):
        pr2(j).wait_recv()
        total = gs[j, x] + rp1[j, 0].astype(F32) + rp2[j].astype(F32)
        part[j] = total
        sz[j] = total.astype(BF16)

        @pl.when(z != 0)
        def _():
            to_column(j, z).start()

    def reduce4(j):
        @pl.when(z == 0)
        def _():
            total = part[j]
            for n in range(1, NZ):
                to_column(j, n).wait_recv()
                total = total + rz[j, n - 1].astype(F32)
            part[j] = total
            sy[j] = total.astype(BF16)

            @pl.when(y != 0)
            def _():
                to_root(j, y).start()

    def reduce5(j):
        @pl.when(top_row)
        def _():
            total = part[j]
            for n in range(1, NY):
                to_root(j, n).wait_recv()
                total = total + ry[j, n - 1].astype(F32)
            part[j] = total

            @pl.when(core == 1)
            def _():
                hand_over(j).start()

    def own_result(j):
        own2(j).wait_recv()
        cols = pl.ds(j * D, D)
        total = g[j, 4 + x] + ro1[j, 0].astype(F32) + ro2[j].astype(F32)
        g[j, 4 + x] = total
        dk_ref[:, cols] = total[0].astype(BF16)
        dv_ref[:, cols] = total[1].astype(BF16)

    def root_result(j):
        @pl.when(is_root)
        def _():
            hand_over(j).wait_recv()
            cols = pl.ds(j * D, D)
            dk_ref[:, cols] = (g[j, 4 + x, 0] + part[j]).astype(BF16)
            dv_ref[:, cols] = (g[j, 4 + x, 1] + rv[j]).astype(BF16)

    for j in range(HEADS):
        relay(j)
    own_part(0)
    prompt1(0)
    prompt1(1)
    own_part(1)
    prompt2(0)
    prompt1(2)
    own_part(2)
    prompt3(0)
    prompt2(1)
    prompt1(3)
    own_part(3)
    prompt3(1)
    prompt2(2)
    prompt2(3)
    between = {
        (0, 1): lambda: prompt3(2),
        (0, 3): lambda: prompt3(3),
    }
    for j in range(1, HEADS):
        between[j, 0] = lambda j=j: reduce1(j - 1)
        between[j, 2] = lambda j=j: (reduce2(j - 1), own_reduce2(j - 1))
        between[j, 4] = lambda j=j: reduce3(j - 1)
    for j in range(2, HEADS):
        between[j, 3] = lambda j=j: (reduce4(j - 2), own_result(j - 2))
    for j in range(HEADS):
        prompt_here(j)
        flip_values(j)
        for i, (at, width) in enumerate(TILES):
            prompt_part(j, at, width)
            between.get((j, i), lambda: None)()
        key_terms(j, 0)
        reduce0(j)
        key_terms(j, 4)
        own_reduce1(j)
        take_out(att_s, att_hbm, 0, j)
        between.get((j, 4), lambda: None)()
    last = HEADS - 1
    reduce1(last)
    query_part(0)
    reduce2(last)
    own_reduce2(last)
    query_part(1)
    reduce4(last - 1)
    reduce3(last)
    query_part(2)
    own_result(last - 1)
    query_part(3)
    own_result(last)
    reduce4(last)
    for j in range(HEADS):
        reduce5(j)
        root_result(j)

    for j in range(HEADS):
        for i in range(3):
            x_send(j, 4, s_own, r_own, i).wait_send()

        @pl.when(core == 0)
        def _():
            for i in range(3):
                x_send(j, 0, s_pr, r_pr, i).wait_send()
            core_send(j).wait_send()

        @pl.when(column)
        def _():
            for n in range(1, NZ):
                z_send(j, n).wait_send()

        @pl.when(is_root)
        def _():
            for n in range(1, NY):
                y_send(j, n).wait_send()

        for copy in (own1(j), own2(j), pair(j), pr1(j), pr2(j)):
            copy.wait_send()

        @pl.when(z != 0)
        def _():
            to_column(j, z).wait_send()

        @pl.when((z == 0) & (y != 0))
        def _():
            to_root(j, y).wait_send()

        @pl.when(root_pair)
        def _():
            hand_over(j).wait_send()

        pltpu.make_async_copy(att_s.at[j], att_s.at[j], osem.at[0, j]).wait()
        pltpu.make_async_copy(dq_s.at[j], dq_s.at[j], osem.at[1, j]).wait()


def main(mask, k, v, q, c):
    dma, vmem = pltpu.SemaphoreType.DMA, pltpu.VMEM
    block = (D, D)
    wide = jax.ShapeDtypeStruct(q.shape, BF16)
    narrow = jax.ShapeDtypeStruct(k.shape, BF16)
    here = pl.BlockSpec(memory_space=pltpu.VMEM)
    there = pl.BlockSpec(memory_space=pl.ANY)
    return pl.pallas_call(
        main_kernel,
        out_shape=(wide, wide, narrow, narrow),
        in_specs=[pl.BlockSpec(memory_space=pltpu.SMEM), here, here, there, there],
        out_specs=(there, there, here, here),
        scratch_shapes=[
            vmem((HEADS, 8, 2) + block, BF16),
            vmem((HEADS, WIDE, D), BF16),
            vmem((HEADS, WIDE, D), BF16),
            vmem((HEADS, WIDE, D), BF16),
            vmem((HEADS, WIDE, D), BF16),
            vmem((4 * D, 2 * D), F32),
            vmem((HEADS, 4 * D, WIDE), F32),
            vmem((HEADS, 4 * D, WIDE), F32),
            vmem((HEADS, 1, WIDE), F32),
            vmem((HEADS, 1, WIDE), F32),
            vmem((4 * D, 2 * D), F32),
            vmem((4 * D, 2 * D), F32),
            vmem((8 * D, WIDE), BF16),
            vmem((HEADS, 8 * D, WIDE), BF16),
            vmem((D, 8 * D), BF16),
            vmem((HEADS, 8, 2) + block, F32),
            vmem((HEADS, 2, 2) + block, BF16),
            vmem((HEADS, 2, 2) + block, BF16),
            vmem((HEADS, 2) + block, BF16),
            vmem((HEADS, 2) + block, BF16),
            vmem((HEADS, 4) + block, BF16),
            vmem((HEADS, 4) + block, BF16),
            vmem((HEADS, 4) + block, F32),
            vmem((HEADS, 2) + block, BF16),
            vmem((HEADS, 2) + block, BF16),
            vmem((HEADS,) + block, BF16),
            vmem((HEADS,) + block, BF16),
            vmem((HEADS,) + block, F32),
            vmem((HEADS,) + block, BF16),
            vmem((HEADS, NZ - 1) + block, BF16),
            vmem((HEADS,) + block, BF16),
            vmem((HEADS, NY - 1) + block, BF16),
            vmem((HEADS,) + block, F32),
            dma((2, HEADS, 2)),
            dma((2, HEADS)),
            dma((2, HEADS)),
            dma((HEADS, 3)),
            dma((HEADS, 3)),
            dma((HEADS, 3)),
            dma((HEADS, 3)),
            dma((HEADS, NY - 1)),
            dma((HEADS, NZ - 1)),
            dma((HEADS,)),
            dma((HEADS,)),
            dma((HEADS,)),
            dma((5, HEADS)),
            dma((5, HEADS)),
            dma((HEADS,)),
            dma((HEADS, NY - 1)),
            dma((HEADS,)),
            dma((HEADS, NZ - 1)),
            dma((HEADS,)),
            dma((HEADS,)),
        ],
        compiler_params=pltpu.CompilerParams(
            collective_id=0, has_side_effects=True, vmem_limit_bytes=60 * 2**20
        ),
        name="tree_attention",
    )(mask, k, v, q, c)


def hand_on_kernel(*refs):
    for src, dst in zip(refs[:4], refs[4:]):
        dst[...] = src[...]


def hand_on(arrays):
    specs = [pl.BlockSpec((D // 4, a.shape[1]), lambda i: (i, 0)) for a in arrays]
    return pl.pallas_call(
        hand_on_kernel,
        grid=(4,),
        out_shape=[jax.ShapeDtypeStruct(a.shape, a.dtype) for a in arrays],
        in_specs=specs,
        out_specs=specs,
        name="hand_on",
    )(*arrays)


def on_device(queries, rotated_key_rows, value_matrix, cotangent, tree_mask):
    return tuple(hand_on(main(tree_mask, rotated_key_rows, value_matrix, queries, cotangent)))


def solution(mesh):
    rows = P(("seq", "head"), None)
    return jax.shard_map(
        on_device,
        mesh=mesh,
        in_specs=(rows, rows, rows, rows, P("seq", None)),
        out_specs=(rows, rows, rows, rows),
        check_vma=False,
    )
```

time: 101 us -> 84.2 us (0.83); the launches traced: 99.1 us -> 84.1 us
  Pallas kernels: 95.3 us -> 83.3 us
  local copies, waits for them, and re-layouts: 3.14 us -> 0 us
    pallas_call x3 -> x2, Pallas kernels: 95.3 us -> 83.3 us  [the longest x1 79.5 us: main(): pl.pallas_call(main_kernel, out_shape=(wide, wide, narrow, narrow), in_sp...]
    unnamed x2 -> x0, local copies, waits for them, and re-layouts: 3.14 us -> none
where the time goes in v2:
time: 84.2 us; the launch traced here: 84.1 us
  Pallas kernels  83.3 us (99%)
    pallas_call x1, Pallas kernels, main(): pl.pallas_call(main_kernel, out_shape=(wide, wide, narrow, narrow), in_sp...  79.5 us
    pallas_call x1, Pallas kernels, hand_on(): pl.pallas_call(hand_on_kernel, grid=(4,), out_shape=[jax.ShapeDtypeStruct...  3.74 us

profile of v2, /device:TPU:2, one launch (start us, length us, event | category | flops | bytes accessed | tf_op | source)
XLA Modules:
  0.0 84.1 jit_solution(8284688199774095368)
XLA Ops:
  0.6 79.5 %tree_attention.1 = (bf16[128,3584]{1,0:T(8,128)(2,1)}, bf16[128,3584]{1,0:T(8,128)(2,1)}, bf16[128,512]{1,0:T(8,128)(2,1)}, bf16[128,512]{1,0:T(8,128)(2,1)}) custom-call(s32[4,4]{1,0:T(4,128)} %mask_ref.1, bf16[128,512]{1,0:T(8,128)(2,1)} %k_ref.1, bf16[128,512]{1,0:T(8,128)(2,1)} %v_ref.1, bf16[128,3584]{1,0:T(8,128)(2,1)} %q_hbm.1, bf16[128,3584]{1,0:T(8,128)(2,1)} %c_hbm.1), custom_call_target="tpu_custom_call" | custom-call | tf_op jit(solution)/shard_map/tree_attention/pallas_call | solution.py:533
  80.2 3.7 %hand_on.1 = (bf16[128,3584]{1,0:T(8,128)(2,1)}, bf16[128,3584]{1,0:T(8,128)(2,1)}, bf16[128,512]{1,0:T(8,128)(2,1)}, bf16[128,512]{1,0:T(8,128)(2,1)}) custom-call(bf16[128,3584]{1,0:T(8,128)(2,1)} %get-tuple-element.8.refs_0_, bf16[128,3584]{1,0:T(8,128)(2,1)} %get-tuple-element.9.refs_1_, bf16[128,512]{1,0:T(8,128)(2,1)} %get-tuple-element.10.refs_2_, ...), custom_call_target="tpu_custom_call" | custom-call | tf_op jit(solution)/shard_map/hand_on/pallas_call | solution.py:607

commit v3 on v2

--- a/solution.py
+++ b/solution.py
@@ -43,35 +43,43 @@
     return (flip, mirror) if j % 2 == 0 else (mirror, flip)
 
 
-def signal(sem, targets):
-    for target in targets:
-        pl.semaphore_signal(sem, inc=1, device_id=target, device_id_type=MESH)
-
-
-def greet(x, y, z, core, tree):
+def others(x):
+    return (x + 1 - 2 * (x % 2), 3 - x, (x + 2) % 4)
+
+
+def say_hello(x, y, z, core):
     sem = pltpu.get_barrier_semaphore()
-    column, leaf, top = tree & (z == 0), tree & (z != 0), tree & (z == 0) & (y == 0)
-    child = tree & (z == 0) & (y != 0)
-
-    @pl.when(top)
-    def _():
-        signal(sem, [device(x, n, 0, core) for n in (2, 1, 3)])
-
-    @pl.when(column)
-    def _():
-        signal(sem, [device(x, y, n, core) for n in (4, 3, 5, 2, 6, 1, 7)])
-
-    @pl.when(child)
-    def _():
-        signal(sem, [device(x, 0, 0, core)])
-
-    @pl.when(leaf)
-    def _():
-        signal(sem, [device(x, y, 0, core)])
-
-    pa, pb = partners(x, 0)
-    signal(sem, [device(pa, y, z, core), device(pb, y, z, core), device(x, y, z, 1 - core)])
-    for role, peers in ((top, 2 + NZ + NY - 1), (child, 2 + NZ + 1), (leaf, 4), (~(column | leaf), 3)):
+
+    def signal(condition, targets):
+        @pl.when(condition)
+        def _():
+            for target in targets:
+                pl.semaphore_signal(sem, inc=1, device_id=target, device_id_type=MESH)
+
+    first = core == 0
+    signal((z == 0) & (y == 0) & first, [device(x, n, 0, c) for n in (2, 1, 3) for c in (0, 1)])
+    signal(z == 0, [device(x, y, n, core) for n in (4, 3, 5, 2, 6, 1, 7)])
+    signal((z == 0) & (y != 0), [device(x, 0, 0, 0)])
+    signal(z != 0, [device(x, y, 0, core)])
+    signal((z == 2) & first, [device(x, y, 3, 0), device(x, y, 4, 0)])
+    signal((z == 6) & first, [device(x, y, 5, 0)])
+    signal(((z == 3) | (z == 4)) & first, [device(x, y, 2, 0)])
+    signal((z == 5) & first, [device(x, y, 6, 0)])
+    signal(z >= 0, [device(n, y, z, core) for n in others(x)] + [device(x, y, z, 1 - core)])
+
+
+def hear_all(x, y, z, core):
+    sem = pltpu.get_barrier_semaphore()
+    first = core == 0
+    end = (z == 1) | (z == 7)
+    for role, peers in (
+        ((z == 0) & (y == 0) & first, 17),
+        ((z == 0) & (y == 0) & ~first, 11),
+        ((z == 0) & (y != 0), 12),
+        ((z != 0) & (~first | end), 5),
+        ((z == 2) & first, 7),
+        ((z != 0) & (z != 2) & ~end & first, 6),
+    ):
         @pl.when(role)
         def _():
             pl.semaphore_wait(sem, peers)
@@ -101,19 +109,20 @@
 def main_kernel(
     mask_ref, k_ref, v_ref, q_hbm, c_hbm,
     att_hbm, dq_hbm, dk_ref, dv_ref,
-    kv, q_s, c_s, att_s, dq_s, bias, po, dpo, mo, lo, sp, dpp, ps, dss, vt,
-    g, so1, ro1, so2, ro2, sc, rc, gs, sp1, rp1, sp2, rp2, part, sz, rz, sy, ry, rv,
+    kv, q_s, c_s, att_s, dq_s, bias, po, dpo, mo, lo, fo, de, sp, dpp, ps, dss, vt,
+    g, so1, ro1, so2, ro2, sc, rc, gs, sp1, rp1, part, sz, rz, sy, ry,
     lsem, qsem, osem, s_own, r_own, s_pr, r_pr, s_by, s_bz, r_t, s_c, r_c,
-    ss, rs, s_y, r_y, s_z, r_z, s_v, r_v,
+    ss, rs, s_a, r_a, s_y, r_y, s_z, r_z,
 ):
     x, y, z, core = place()
     opp = (x + 2) % 4
     seq = lax.axis_index("seq")
     top_row = (z == 0) & (y == 0)
     is_root = top_row & (core == 0)
-    root_pair = top_row & (core == 1)
     column = (core == 0) & (z == 0)
     leaf = (core == 0) & (z != 0)
+
+    say_hello(x, y, z, core)
 
     def local(j, block, base):
         return [
@@ -121,10 +130,6 @@
             for t, ref in enumerate((k_ref, v_ref))
         ]
 
-    for j in range(HEADS):
-        for copy in local(j, 4 + x, 0):
-            copy.start()
-
     @pl.when(is_root)
     def _():
         for j in range(HEADS):
@@ -132,6 +137,10 @@
                 copy.start()
 
     for j in range(HEADS):
+        for copy in local(j, 4 + x, 0):
+            copy.start()
+
+    for j in range(HEADS):
         for h in range(GROUP):
             cols, rows = pl.ds((j * GROUP + h) * D, D), pl.ds(h * D, D)
             pltpu.make_async_copy(q_hbm.at[:, cols], q_s.at[j, rows], qsem.at[0, j]).start()
@@ -142,7 +151,7 @@
             cols, rows = pl.ds((j * GROUP + h) * D, D), pl.ds(h * D, D)
             pltpu.make_async_copy(buf.at[j, rows], hbm.at[:, cols], osem.at[i, j]).start()
 
-    greet(x, y, z, core, z >= 0)
+    hear_all(x, y, z, core)
 
     def y_send(j, n):
         blk = kv.at[j, x]
@@ -151,6 +160,10 @@
     def z_send(j, n):
         blk = kv.at[j, x]
         return remote(blk, blk, s_bz.at[j, n - 1], r_t.at[j], device(x, y, n, 0))
+
+    def pass_on(j):
+        for n in (2, 6, 1, 7):
+            z_send(j, n).start()
 
     def x_send(j, base, ss, rs, i):
         pa, pb = partners(x, j)
@@ -161,6 +174,10 @@
         pa, pb = partners(x, j)
         blk = kv.at[j, base + (pa, pb, opp)[i]]
         remote(blk, blk, ss.at[j, i], rs.at[j, i], device((pa, pb, pb)[i], y, z, core)).wait_recv()
+
+    def p_send(j, i):
+        blk = kv.at[j, x]
+        return remote(blk, blk, s_pr.at[j, i], r_pr.at[j, i], device(others(x)[i], y, z, core))
 
     def core_send(j):
         blk = kv.at[j, pl.ds(0, 4)]
@@ -173,6 +190,7 @@
                 copy.wait()
             for n in (2, 1, 3):
                 y_send(j, n).start()
+            pass_on(j)
 
     for j in range(HEADS):
         for copy in local(j, 4 + x, 0):
@@ -193,39 +211,39 @@
         levels.append(jnp.where(reads > 0, 0.0, -1e30).astype(F32))
 
     def relay(j):
-        @pl.when(column)
-        def _():
-            @pl.when(y != 0)
-            def _():
-                y_send(j, y).wait_recv()
-
-            for n in (4, 5, 3, 6, 2, 7, 1):
-                z_send(j, n).start()
+        @pl.when(column & (y != 0))
+        def _():
+            y_send(j, y).wait_recv()
+            pass_on(j)
 
         x_arrival(j, 4, s_own, r_own, 0)
         x_send(j, 4, s_own, r_own, 2).start()
 
     def prompt1(j):
+        @pl.when(leaf)
+        def _():
+            z_send(j, z).wait_recv()
+
+            @pl.when(z == 2)
+            def _():
+                z_send(j, 4).start()
+                z_send(j, 3).start()
+
+            @pl.when(z == 6)
+            def _():
+                z_send(j, 5).start()
+
         @pl.when(core == 0)
         def _():
-            @pl.when(leaf)
-            def _():
-                z_send(j, z).wait_recv()
-
-            x_send(j, 0, s_pr, r_pr, 0).start()
-            x_send(j, 0, s_pr, r_pr, 1).start()
-
-    def prompt2(j):
-        @pl.when(core == 0)
-        def _():
-            x_arrival(j, 0, s_pr, r_pr, 0)
-            x_send(j, 0, s_pr, r_pr, 2).start()
+            for i in (2, 0, 1):
+                p_send(j, i).start()
 
     def prompt3(j):
         @pl.when(core == 0)
         def _():
-            x_arrival(j, 0, s_pr, r_pr, 1)
-            x_arrival(j, 0, s_pr, r_pr, 2)
+            for i, n in enumerate(others(x)):
+                blk = kv.at[j, n]
+                remote(blk, blk, s_pr.at[j, i], r_pr.at[j, i], device(n, y, z, core)).wait_recv()
             core_send(j).start()
 
     def prompt_here(j):
@@ -284,11 +302,12 @@
         total = jnp.sum(total, axis=0, keepdims=True) + lo[j, :, cols] * shrink
         inverse = 1.0 / total
         shrink = shrink * inverse
+        fo[j, :, cols] = shrink
         for b in range(QUARTERS):
             rows = pl.ds(b * D, D)
-            ps[rows, cols] = (sp[rows, wide] * inverse).astype(BF16)
-            ps[pl.ds((4 + b) * D, D), cols] = (po[j, rows, cols] * shrink).astype(BF16)
-        out_t = nn(vt[...], ps[:, cols]).astype(BF16)
+            ps[j, rows, cols] = (sp[rows, wide] * inverse).astype(BF16)
+            ps[j, pl.ds((4 + b) * D, D), cols] = (po[j, rows, cols] * shrink).astype(BF16)
+        out_t = nn(vt[...], ps[j, :, cols]).astype(BF16)
         deltas = []
         for i in range(width // D):
             lanes, rows = slice(i * D, i * D + D), pl.ds(at + i * D, D)
@@ -296,17 +315,26 @@
             prod = c_s[j, rows, :].T.astype(F32) * out_t[:, lanes].astype(F32)
             deltas.append(jnp.sum(prod, axis=0, keepdims=True))
         delta = jnp.concatenate(deltas, axis=1)
+        de[j, :, cols] = delta
         for b in range(QUARTERS):
             rows = pl.ds(b * D, D)
             dss[j, rows, cols] = ((sp[rows, wide] * inverse) * (dpp[rows, wide] - delta)).astype(BF16)
-            dss[j, pl.ds((4 + b) * D, D), cols] = (
-                (po[j, rows, cols] * shrink) * (dpo[j, rows, cols] - delta)
-            ).astype(BF16)
+
+    def own_terms(j):
+        for at, width in TILES:
+            cols = pl.ds(at, width)
+            for b in range(QUARTERS):
+                rows = pl.ds(b * D, D)
+                dss[j, pl.ds((4 + b) * D, D), cols] = (
+                    (po[j, rows, cols] * fo[j, :, cols]) * (dpo[j, rows, cols] - de[j, :, cols])
+                ).astype(BF16)
+        key_terms(j, 4)
+        own_reduce1(j)
 
     def key_terms(j, first):
         rows = pl.ds(first * D, 4 * D)
         g[j, first : first + 4, 0] = (nn(dss[j, rows, :], q_s[j]) * SCALE).reshape(4, D, D)
-        g[j, first : first + 4, 1] = nn(ps[rows, :], c_s[j]).reshape(4, D, D)
+        g[j, first : first + 4, 1] = nn(ps[j, rows, :], c_s[j]).reshape(4, D, D)
 
     def query_part(j):
         for b in range(2 * QUARTERS):
@@ -329,20 +357,14 @@
     def pair(j):
         return hop(sc, rc, 2, j, device(x, y, z, 1 - core))
 
-    def pr1(j):
-        return hop(sp1, rp1, 3, j, device(partners(x, j)[0], y, z, core))
-
-    def pr2(j):
-        return hop(sp2, rp2, 4, j, device(partners(x, j)[1], y, z, core))
+    def across(j, i):
+        return remote(sp1.at[j, i], rp1.at[j, i], s_a.at[j, i], r_a.at[j, i], device(others(x)[i], y, z, core))
 
     def to_column(j, n):
         return remote(sz.at[j], rz.at[j, n - 1], s_z.at[j], r_z.at[j, n - 1], device(x, y, 0, core))
 
-    def to_root(j, n):
-        return remote(sy.at[j], ry.at[j, n - 1], s_y.at[j], r_y.at[j, n - 1], device(x, 0, 0, core))
-
-    def hand_over(j):
-        return remote(part.at[j], rv.at[j], s_v.at[j], r_v.at[j], device(x, y, z, 1 - core))
+    def to_root(j, t, n):
+        return remote(sy.at[j], ry.at[j, t, n], s_y.at[j], r_y.at[j, t, n], device(x, 0, 0, 0))
 
     def reduce0(j):
         for b in range(QUARTERS):
@@ -356,19 +378,12 @@
         own1(j).start()
 
     def reduce1(j):
-        pa, pb = partners(x, j)
         pair(j).wait_recv()
         for b in range(QUARTERS):
             gs[j, b] = g[j, b, core] + rc[j, b].astype(F32)
-        sp1[j, 0] = gs[j, pa].astype(BF16)
-        sp1[j, 1] = gs[j, opp].astype(BF16)
-        pr1(j).start()
-
-    def reduce2(j):
-        pa, pb = partners(x, j)
-        pr1(j).wait_recv()
-        sp2[j] = (gs[j, pb] + rp1[j, 1].astype(F32)).astype(BF16)
-        pr2(j).start()
+        for i in (2, 0, 1):
+            sp1[j, i] = gs[j, others(x)[i]].astype(BF16)
+            across(j, i).start()
 
     def own_reduce2(j):
         pa, pb = partners(x, j)
@@ -377,8 +392,10 @@
         own2(j).start()
 
     def reduce3(j):
-        pr2(j).wait_recv()
-        total = gs[j, x] + rp1[j, 0].astype(F32) + rp2[j].astype(F32)
+        total = gs[j, x]
+        for i in range(3):
+            across(j, i).wait_recv()
+            total = total + rp1[j, i].astype(F32)
         part[j] = total
         sz[j] = total.astype(BF16)
 
@@ -396,22 +413,9 @@
             part[j] = total
             sy[j] = total.astype(BF16)
 
-            @pl.when(y != 0)
+            @pl.when((y != 0) | (core == 1))
             def _():
-                to_root(j, y).start()
-
-    def reduce5(j):
-        @pl.when(top_row)
-        def _():
-            total = part[j]
-            for n in range(1, NY):
-                to_root(j, n).wait_recv()
-                total = total + ry[j, n - 1].astype(F32)
-            part[j] = total
-
-            @pl.when(core == 1)
-            def _():
-                hand_over(j).start()
+                to_root(j, core, y).start()
 
     def own_result(j):
         own2(j).wait_recv()
@@ -424,37 +428,39 @@
     def root_result(j):
         @pl.when(is_root)
         def _():
-            hand_over(j).wait_recv()
             cols = pl.ds(j * D, D)
-            dk_ref[:, cols] = (g[j, 4 + x, 0] + part[j]).astype(BF16)
-            dv_ref[:, cols] = (g[j, 4 + x, 1] + rv[j]).astype(BF16)
+            total = g[j, 4 + x, 0] + part[j]
+            for n in range(1, NY):
+                to_root(j, 0, n).wait_recv()
+                total = total + ry[j, 0, n].astype(F32)
+            dk_ref[:, cols] = total.astype(BF16)
+            total = g[j, 4 + x, 1]
+            for n in range(NY):
+                to_root(j, 1, n).wait_recv()
+                total = total + ry[j, 1, n].astype(F32)
+            dv_ref[:, cols] = total.astype(BF16)
 
     for j in range(HEADS):
         relay(j)
+    prompt1(0)
     own_part(0)
-    prompt1(0)
     prompt1(1)
     own_part(1)
-    prompt2(0)
     prompt1(2)
     own_part(2)
     prompt3(0)
-    prompt2(1)
+    own_part(3)
     prompt1(3)
-    own_part(3)
-    prompt3(1)
-    prompt2(2)
-    prompt2(3)
     between = {
-        (0, 1): lambda: prompt3(2),
-        (0, 3): lambda: prompt3(3),
+        (0, 0): lambda: prompt3(1),
+        (0, 2): lambda: prompt3(2),
+        (1, 0): lambda: prompt3(3),
+        (1, 2): lambda: reduce1(0),
+        (2, 1): lambda: reduce1(1),
+        (2, 3): lambda: reduce3(0),
+        (3, 1): lambda: reduce1(2),
+        (3, 3): lambda: reduce3(1),
     }
-    for j in range(1, HEADS):
-        between[j, 0] = lambda j=j: reduce1(j - 1)
-        between[j, 2] = lambda j=j: (reduce2(j - 1), own_reduce2(j - 1))
-        between[j, 4] = lambda j=j: reduce3(j - 1)
-    for j in range(2, HEADS):
-        between[j, 3] = lambda j=j: (reduce4(j - 2), own_result(j - 2))
     for j in range(HEADS):
         prompt_here(j)
         flip_values(j)
@@ -463,25 +469,31 @@
             between.get((j, i), lambda: None)()
         key_terms(j, 0)
         reduce0(j)
-        key_terms(j, 4)
-        own_reduce1(j)
         take_out(att_s, att_hbm, 0, j)
-        between.get((j, 4), lambda: None)()
-    last = HEADS - 1
-    reduce1(last)
+    own_terms(0)
+    reduce1(3)
+    own_terms(1)
+    reduce3(2)
+    own_terms(2)
+    own_terms(3)
+    reduce3(3)
+    reduce4(0)
+    own_reduce2(0)
     query_part(0)
-    reduce2(last)
-    own_reduce2(last)
+    reduce4(1)
+    own_reduce2(1)
     query_part(1)
-    reduce4(last - 1)
-    reduce3(last)
+    reduce4(2)
+    own_reduce2(2)
     query_part(2)
-    own_result(last - 1)
+    own_reduce2(3)
     query_part(3)
-    own_result(last)
-    reduce4(last)
+    own_result(0)
+    own_result(1)
+    reduce4(3)
+    own_result(2)
+    own_result(3)
     for j in range(HEADS):
-        reduce5(j)
         root_result(j)
 
     for j in range(HEADS):
@@ -491,33 +503,38 @@
         @pl.when(core == 0)
         def _():
             for i in range(3):
-                x_send(j, 0, s_pr, r_pr, i).wait_send()
+                p_send(j, i).wait_send()
             core_send(j).wait_send()
 
         @pl.when(column)
         def _():
-            for n in range(1, NZ):
+            for n in (2, 6, 1, 7):
                 z_send(j, n).wait_send()
+
+        @pl.when(leaf & (z == 2))
+        def _():
+            z_send(j, 4).wait_send()
+            z_send(j, 3).wait_send()
+
+        @pl.when(leaf & (z == 6))
+        def _():
+            z_send(j, 5).wait_send()
 
         @pl.when(is_root)
         def _():
             for n in range(1, NY):
                 y_send(j, n).wait_send()
 
-        for copy in (own1(j), own2(j), pair(j), pr1(j), pr2(j)):
+        for copy in (own1(j), own2(j), pair(j), across(j, 0), across(j, 1), across(j, 2)):
             copy.wait_send()
 
         @pl.when(z != 0)
         def _():
             to_column(j, z).wait_send()
 
-        @pl.when((z == 0) & (y != 0))
-        def _():
-            to_root(j, y).wait_send()
-
-        @pl.when(root_pair)
-        def _():
-            hand_over(j).wait_send()
+        @pl.when((z == 0) & ((y != 0) | (core == 1)))
+        def _():
+            to_root(j, core, y).wait_send()
 
         pltpu.make_async_copy(att_s.at[j], att_s.at[j], osem.at[0, j]).wait()
         pltpu.make_async_copy(dq_s.at[j], dq_s.at[j], osem.at[1, j]).wait()
@@ -533,7 +550,7 @@
     return pl.pallas_call(
         main_kernel,
         out_shape=(wide, wide, narrow, narrow),
-        in_specs=[pl.BlockSpec(memory_space=pltpu.SMEM), here, here, there, there],
+        in_specs=[pl.BlockSpec(memory_space=pltpu.SMEM), there, there, there, there],
         out_specs=(there, there, here, here),
         scratch_shapes=[
             vmem((HEADS, 8, 2) + block, BF16),
@@ -546,9 +563,11 @@
             vmem((HEADS, 4 * D, WIDE), F32),
             vmem((HEADS, 1, WIDE), F32),
             vmem((HEADS, 1, WIDE), F32),
+            vmem((HEADS, 1, WIDE), F32),
+            vmem((HEADS, 1, WIDE), F32),
             vmem((4 * D, 2 * D), F32),
             vmem((4 * D, 2 * D), F32),
-            vmem((8 * D, WIDE), BF16),
+            vmem((HEADS, 8 * D, WIDE), BF16),
             vmem((HEADS, 8 * D, WIDE), BF16),
             vmem((D, 8 * D), BF16),
             vmem((HEADS, 8, 2) + block, F32),
@@ -559,16 +578,13 @@
             vmem((HEADS, 4) + block, BF16),
             vmem((HEADS, 4) + block, BF16),
             vmem((HEADS, 4) + block, F32),
-            vmem((HEADS, 2) + block, BF16),
-            vmem((HEADS, 2) + block, BF16),
-            vmem((HEADS,) + block, BF16),
-            vmem((HEADS,) + block, BF16),
+            vmem((HEADS, 3) + block, BF16),
+            vmem((HEADS, 3) + block, BF16),
             vmem((HEADS,) + block, F32),
             vmem((HEADS,) + block, BF16),
             vmem((HEADS, NZ - 1) + block, BF16),
             vmem((HEADS,) + block, BF16),
-            vmem((HEADS, NY - 1) + block, BF16),
-            vmem((HEADS,) + block, F32),
+            vmem((HEADS, 2, NY) + block, BF16),
             dma((2, HEADS, 2)),
             dma((2, HEADS)),
             dma((2, HEADS)),
@@ -581,14 +597,14 @@
             dma((HEADS,)),
             dma((HEADS,)),
             dma((HEADS,)),
-            dma((5, HEADS)),
-            dma((5, HEADS)),
+            dma((3, HEADS)),
+            dma((3, HEADS)),
+            dma((HEADS, 3)),
+            dma((HEADS, 3)),
             dma((HEADS,)),
-            dma((HEADS, NY - 1)),
+            dma((HEADS, 2, NY)),
             dma((HEADS,)),
             dma((HEADS, NZ - 1)),
-            dma((HEADS,)),
-            dma((HEADS,)),
         ],
         compiler_params=pltpu.CompilerParams(
             collective_id=0, has_side_effects=True, vmem_limit_bytes=60 * 2**20
@@ -597,19 +613,39 @@
     )(mask, k, v, q, c)
 
 
+PIECES = 2
+
+
 def hand_on_kernel(*refs):
-    for src, dst in zip(refs[:4], refs[4:]):
-        dst[...] = src[...]
+    arrays, outs, held, (came, went) = refs[:4], refs[4:8], refs[8:12], refs[12:]
+
+    def copies(i, p):
+        rows = pl.ds(p * (D // PIECES), D // PIECES)
+        inner = held[i].at[rows]
+        return (
+            pltpu.make_async_copy(arrays[i].at[rows], inner, came.at[i, p]),
+            pltpu.make_async_copy(inner, outs[i].at[rows], went.at[i, p]),
+        )
+
+    order = [(i, p) for i in (2, 3, 0, 1) for p in range(PIECES)]
+    for at in order:
+        copies(*at)[0].start()
+    for at in order:
+        copies(*at)[0].wait()
+        copies(*at)[1].start()
+    for at in order:
+        copies(*at)[1].wait()
 
 
 def hand_on(arrays):
-    specs = [pl.BlockSpec((D // 4, a.shape[1]), lambda i: (i, 0)) for a in arrays]
+    there = pl.BlockSpec(memory_space=pl.ANY)
     return pl.pallas_call(
         hand_on_kernel,
-        grid=(4,),
         out_shape=[jax.ShapeDtypeStruct(a.shape, a.dtype) for a in arrays],
-        in_specs=specs,
-        out_specs=specs,
+        in_specs=[there] * 4,
+        out_specs=[there] * 4,
+        scratch_shapes=[pltpu.VMEM(a.shape, a.dtype) for a in arrays]
+        + [pltpu.SemaphoreType.DMA((4, PIECES))] * 2,
         name="hand_on",
     )(*arrays)
 

time: 84.2 us -> 62 us (0.74)
  Pallas kernels: 83.3 us -> 61 us
    pallas_call x1, Pallas kernels: 79.5 us -> 58.5 us  [main(): pl.pallas_call(main_kernel, out_shape=(wide, wide, narrow, narrow), in_sp...]
    pallas_call x1, Pallas kernels: 3.74 us -> 2.52 us  [hand_on(): pl.pallas_call(hand_on_kernel, out_shape=[jax.ShapeDtypeStruct(a.shape, a...]
where the time goes in v3:
time: 62 us; the launch traced here: 61.8 us
  Pallas kernels  61 us (98%)
  between operations  0.8 us (1%)
    pallas_call x1, Pallas kernels, main(): pl.pallas_call(main_kernel, out_shape=(wide, wide, narrow, narrow), in_sp...  58.5 us
    pallas_call x1, Pallas kernels, hand_on(): pl.pallas_call(hand_on_kernel, out_shape=[jax.ShapeDtypeStruct(a.shape, a...  2.52 us

profile of v3, /device:TPU:2, one launch (start us, length us, event | category | flops | bytes accessed | tf_op | source)
XLA Modules:
  0.0 61.8 jit_solution(2849251838353654971)
XLA Ops:
  0.6 58.5 %tree_attention.1 = (bf16[128,3584]{1,0:T(8,128)(2,1)}, bf16[128,3584]{1,0:T(8,128)(2,1)}, bf16[128,512]{1,0:T(8,128)(2,1)}, bf16[128,512]{1,0:T(8,128)(2,1)}) custom-call(s32[4,4]{1,0:T(4,128)} %mask_ref.1, bf16[128,512]{1,0:T(8,128)(2,1)} %k_ref.1, bf16[128,512]{1,0:T(8,128)(2,1)} %v_ref.1, bf16[128,3584]{1,0:T(8,128)(2,1)} %q_hbm.1, bf16[128,3584]{1,0:T(8,128)(2,1)} %c_hbm.1), custom_call_target="tpu_custom_call" | custom-call | tf_op jit(solution)/shard_map/tree_attention/pallas_call | solution.py:550
  59.1 2.5 %hand_on.1 = (bf16[128,3584]{1,0:T(8,128)(2,1)}, bf16[128,3584]{1,0:T(8,128)(2,1)}, bf16[128,512]{1,0:T(8,128)(2,1)}, bf16[128,512]{1,0:T(8,128)(2,1)}) custom-call(bf16[128,3584]{1,0:T(8,128)(2,1)} %get-tuple-element.8.refs_0_, bf16[128,3584]{1,0:T(8,128)(2,1)} %get-tuple-element.9.refs_1_, bf16[128,512]{1,0:T(8,128)(2,1)} %get-tuple-element.10.refs_2_, ...), custom_call_target="tpu_custom_call" | custom-call | tf_op jit(solution)/shard_map/hand_on/pallas_call | solution.py:642

commit v4 on v3

--- a/solution.py
+++ b/solution.py
@@ -140,12 +140,6 @@
         for copy in local(j, 4 + x, 0):
             copy.start()
 
-    for j in range(HEADS):
-        for h in range(GROUP):
-            cols, rows = pl.ds((j * GROUP + h) * D, D), pl.ds(h * D, D)
-            pltpu.make_async_copy(q_hbm.at[:, cols], q_s.at[j, rows], qsem.at[0, j]).start()
-            pltpu.make_async_copy(c_hbm.at[:, cols], c_s.at[j, rows], qsem.at[1, j]).start()
-
     def take_out(buf, hbm, i, j):
         for h in range(GROUP):
             cols, rows = pl.ds((j * GROUP + h) * D, D), pl.ds(h * D, D)
@@ -161,8 +155,11 @@
         blk = kv.at[j, x]
         return remote(blk, blk, s_bz.at[j, n - 1], r_t.at[j], device(x, y, n, 0))
 
+    def children(j):
+        return (4, 5, 3, 6, 2, 7, 1) if j == 0 else (2, 6, 1, 7)
+
     def pass_on(j):
-        for n in (2, 6, 1, 7):
+        for n in children(j):
             z_send(j, n).start()
 
     def x_send(j, base, ss, rs, i):
@@ -179,9 +176,14 @@
         blk = kv.at[j, x]
         return remote(blk, blk, s_pr.at[j, i], r_pr.at[j, i], device(others(x)[i], y, z, core))
 
-    def core_send(j):
-        blk = kv.at[j, pl.ds(0, 4)]
-        return remote(blk, blk, s_c.at[j], r_c.at[j], device(x, y, z, 1 - core))
+    def core_send(j, i):
+        blk = kv.at[j, x if i == 3 else others(x)[i]]
+        return remote(blk, blk, s_c.at[j, i], r_c.at[j, i], device(x, y, z, 1 - core))
+
+    def spread(j):
+        for i in (2, 0, 1):
+            p_send(j, i).start()
+        core_send(j, 3).start()
 
     @pl.when(is_root)
     def _():
@@ -191,12 +193,19 @@
             for n in (2, 1, 3):
                 y_send(j, n).start()
             pass_on(j)
+            spread(j)
 
     for j in range(HEADS):
         for copy in local(j, 4 + x, 0):
             copy.wait()
         x_send(j, 4, s_own, r_own, 0).start()
         x_send(j, 4, s_own, r_own, 1).start()
+
+    for j in range(HEADS):
+        for h in range(GROUP):
+            cols, rows = pl.ds((j * GROUP + h) * D, D), pl.ds(h * D, D)
+            pltpu.make_async_copy(q_hbm.at[:, cols], q_s.at[j, rows], qsem.at[0, j]).start()
+            pltpu.make_async_copy(c_hbm.at[:, cols], c_s.at[j, rows], qsem.at[1, j]).start()
 
     key = lax.broadcasted_iota(jnp.int32, (D, D), 0)
     query = lax.broadcasted_iota(jnp.int32, (D, D), 1)
@@ -215,41 +224,40 @@
         def _():
             y_send(j, y).wait_recv()
             pass_on(j)
+            spread(j)
 
         x_arrival(j, 4, s_own, r_own, 0)
         x_send(j, 4, s_own, r_own, 2).start()
 
-    def prompt1(j):
-        @pl.when(leaf)
+    def prompt1(j, here):
+        @pl.when(here)
         def _():
             z_send(j, z).wait_recv()
-
-            @pl.when(z == 2)
-            def _():
-                z_send(j, 4).start()
-                z_send(j, 3).start()
-
-            @pl.when(z == 6)
-            def _():
-                z_send(j, 5).start()
-
-        @pl.when(core == 0)
-        def _():
-            for i in (2, 0, 1):
-                p_send(j, i).start()
+            if j > 0:
+                @pl.when(z == 2)
+                def _():
+                    z_send(j, 4).start()
+                    z_send(j, 3).start()
+
+                @pl.when(z == 6)
+                def _():
+                    z_send(j, 5).start()
+
+            spread(j)
 
     def prompt3(j):
         @pl.when(core == 0)
         def _():
-            for i, n in enumerate(others(x)):
-                blk = kv.at[j, n]
-                remote(blk, blk, s_pr.at[j, i], r_pr.at[j, i], device(n, y, z, core)).wait_recv()
-            core_send(j).start()
+            for i in (0, 1, 2):
+                blk = kv.at[j, others(x)[i]]
+                remote(blk, blk, s_pr.at[j, i], r_pr.at[j, i], device(others(x)[i], y, z, core)).wait_recv()
+                core_send(j, i).start()
 
     def prompt_here(j):
         @pl.when(core == 1)
         def _():
-            core_send(j).wait_recv()
+            for i in range(4):
+                core_send(j, i).wait_recv()
 
     def own_part(j):
         x_arrival(j, 4, s_own, r_own, 1)
@@ -329,7 +337,6 @@
                     (po[j, rows, cols] * fo[j, :, cols]) * (dpo[j, rows, cols] - de[j, :, cols])
                 ).astype(BF16)
         key_terms(j, 4)
-        own_reduce1(j)
 
     def key_terms(j, first):
         rows = pl.ds(first * D, 4 * D)
@@ -440,17 +447,25 @@
                 total = total + ry[j, 1, n].astype(F32)
             dv_ref[:, cols] = total.astype(BF16)
 
-    for j in range(HEADS):
-        relay(j)
-    prompt1(0)
+    near = leaf & ((z < 3) | (z > 5))
+    far = leaf & (z > 2) & (z < 6)
+    relay(0)
+    relay(1)
+    prompt1(0, near)
+    relay(2)
+    relay(3)
+    prompt1(0, far)
+    prompt1(1, near)
     own_part(0)
-    prompt1(1)
+    prompt1(1, far)
+    prompt1(2, near)
     own_part(1)
-    prompt1(2)
+    prompt1(2, far)
+    prompt1(3, near)
     own_part(2)
     prompt3(0)
     own_part(3)
-    prompt1(3)
+    prompt1(3, far)
     between = {
         (0, 0): lambda: prompt3(1),
         (0, 2): lambda: prompt3(2),
@@ -472,25 +487,29 @@
         take_out(att_s, att_hbm, 0, j)
     own_terms(0)
     reduce1(3)
+    own_reduce1(0)
+    reduce3(2)
     own_terms(1)
-    reduce3(2)
+    own_reduce1(1)
     own_terms(2)
+    own_reduce1(2)
+    reduce4(0)
     own_terms(3)
     reduce3(3)
-    reduce4(0)
+    own_reduce1(3)
     own_reduce2(0)
+    reduce4(1)
     query_part(0)
-    reduce4(1)
     own_reduce2(1)
+    reduce4(2)
     query_part(1)
-    reduce4(2)
     own_reduce2(2)
     query_part(2)
+    query_part(3)
+    reduce4(3)
     own_reduce2(3)
-    query_part(3)
     own_result(0)
     own_result(1)
-    reduce4(3)
     own_result(2)
     own_result(3)
     for j in range(HEADS):
@@ -504,21 +523,23 @@
         def _():
             for i in range(3):
                 p_send(j, i).wait_send()
-            core_send(j).wait_send()
+            for i in range(4):
+                core_send(j, i).wait_send()
 
         @pl.when(column)
         def _():
-            for n in (2, 6, 1, 7):
+            for n in children(j):
                 z_send(j, n).wait_send()
 
-        @pl.when(leaf & (z == 2))
-        def _():
-            z_send(j, 4).wait_send()
-            z_send(j, 3).wait_send()
-
-        @pl.when(leaf & (z == 6))
-        def _():
-            z_send(j, 5).wait_send()
+        if j > 0:
+            @pl.when(leaf & (z == 2))
+            def _():
+                z_send(j, 4).wait_send()
+                z_send(j, 3).wait_send()
+
+            @pl.when(leaf & (z == 6))
+            def _():
+                z_send(j, 5).wait_send()
 
         @pl.when(is_root)
         def _():
@@ -595,8 +616,8 @@
             dma((HEADS, NY - 1)),
             dma((HEADS, NZ - 1)),
             dma((HEADS,)),
-            dma((HEADS,)),
-            dma((HEADS,)),
+            dma((HEADS, 4)),
+            dma((HEADS, 4)),
             dma((3, HEADS)),
             dma((3, HEADS)),
             dma((HEADS, 3)),

time: 62 us -> 62.4 us (level)
  no operation moved by 1% of the time
where the time goes in v4:
time: 62.4 us; the launch traced here: 62.2 us
  Pallas kernels  61.4 us (98%)
  between operations  0.8 us (1%)
    pallas_call x1, Pallas kernels, main(): pl.pallas_call(main_kernel, out_shape=(wide, wide, narrow, narrow), in_sp...  58.9 us
    pallas_call x1, Pallas kernels, hand_on(): pl.pallas_call(hand_on_kernel, out_shape=[jax.ShapeDtypeStruct(a.shape, a...  2.52 us

profile of v4, /device:TPU:2, one launch (start us, length us, event | category | flops | bytes accessed | tf_op | source)
XLA Modules:
  0.0 62.2 jit_solution(7491391102747976837)
XLA Ops:
  0.6 58.9 %tree_attention.1 = (bf16[128,3584]{1,0:T(8,128)(2,1)}, bf16[128,3584]{1,0:T(8,128)(2,1)}, bf16[128,512]{1,0:T(8,128)(2,1)}, bf16[128,512]{1,0:T(8,128)(2,1)}) custom-call(s32[4,4]{1,0:T(4,128)} %mask_ref.1, bf16[128,512]{1,0:T(8,128)(2,1)} %k_ref.1, bf16[128,512]{1,0:T(8,128)(2,1)} %v_ref.1, bf16[128,3584]{1,0:T(8,128)(2,1)} %q_hbm.1, bf16[128,3584]{1,0:T(8,128)(2,1)} %c_hbm.1), custom_call_target="tpu_custom_call" | custom-call | tf_op jit(solution)/shard_map/tree_attention/pallas_call | solution.py:571
  59.6 2.5 %hand_on.1 = (bf16[128,3584]{1,0:T(8,128)(2,1)}, bf16[128,3584]{1,0:T(8,128)(2,1)}, bf16[128,512]{1,0:T(8,128)(2,1)}, bf16[128,512]{1,0:T(8,128)(2,1)}) custom-call(bf16[128,3584]{1,0:T(8,128)(2,1)} %get-tuple-element.8.refs_0_, bf16[128,3584]{1,0:T(8,128)(2,1)} %get-tuple-element.9.refs_1_, bf16[128,512]{1,0:T(8,128)(2,1)} %get-tuple-element.10.refs_2_, ...), custom_call_target="tpu_custom_call" | custom-call | tf_op jit(solution)/shard_map/hand_on/pallas_call | solution.py:663

commit v5 on v4

--- a/solution.py
+++ b/solution.py
@@ -121,6 +121,7 @@
     is_root = top_row & (core == 0)
     column = (core == 0) & (z == 0)
     leaf = (core == 0) & (z != 0)
+    mesh_c0 = (core == 0) & ~top_row
 
     say_hello(x, y, z, core)
 
@@ -133,8 +134,9 @@
     @pl.when(is_root)
     def _():
         for j in range(HEADS):
-            for copy in local(j, x, 1):
-                copy.start()
+            for b in range(QUARTERS):
+                for copy in local(j, b, 1 + b):
+                    copy.start()
 
     for j in range(HEADS):
         for copy in local(j, 4 + x, 0):
@@ -156,7 +158,7 @@
         return remote(blk, blk, s_bz.at[j, n - 1], r_t.at[j], device(x, y, n, 0))
 
     def children(j):
-        return (4, 5, 3, 6, 2, 7, 1) if j == 0 else (2, 6, 1, 7)
+        return (4, 5, 3, 6, 2, 7, 1) if j < 2 else (2, 6, 1, 7)
 
     def pass_on(j):
         for n in children(j):
@@ -176,9 +178,10 @@
         blk = kv.at[j, x]
         return remote(blk, blk, s_pr.at[j, i], r_pr.at[j, i], device(others(x)[i], y, z, core))
 
-    def core_send(j, i):
-        blk = kv.at[j, x if i == 3 else others(x)[i]]
-        return remote(blk, blk, s_c.at[j, i], r_c.at[j, i], device(x, y, z, 1 - core))
+    def core_send(j, i, base=0):
+        n = x if i == 3 else others(x)[i]
+        src, dst = kv.at[j, base + n], kv.at[j, n]
+        return remote(src, dst, s_c.at[j, i], r_c.at[j, i], device(x, y, z, 1 - core))
 
     def spread(j):
         for i in (2, 0, 1):
@@ -188,12 +191,13 @@
     @pl.when(is_root)
     def _():
         for j in range(HEADS):
-            for copy in local(j, x, 1):
-                copy.wait()
+            for b in range(QUARTERS):
+                for copy in local(j, b, 1 + b):
+                    copy.wait()
             for n in (2, 1, 3):
                 y_send(j, n).start()
             pass_on(j)
-            spread(j)
+            core_send(j, 3).start()
 
     for j in range(HEADS):
         for copy in local(j, 4 + x, 0):
@@ -233,7 +237,7 @@
         @pl.when(here)
         def _():
             z_send(j, z).wait_recv()
-            if j > 0:
+            if j > 1:
                 @pl.when(z == 2)
                 def _():
                     z_send(j, 4).start()
@@ -246,7 +250,12 @@
             spread(j)
 
     def prompt3(j):
-        @pl.when(core == 0)
+        @pl.when(is_root)
+        def _():
+            for i in (0, 1, 2):
+                core_send(j, i, 4).start()
+
+        @pl.when(mesh_c0)
         def _():
             for i in (0, 1, 2):
                 blk = kv.at[j, others(x)[i]]
@@ -457,17 +466,16 @@
     prompt1(0, far)
     prompt1(1, near)
     own_part(0)
+    own_part(1)
     prompt1(1, far)
+    own_part(2)
     prompt1(2, near)
-    own_part(1)
+    prompt3(0)
+    own_part(3)
     prompt1(2, far)
     prompt1(3, near)
-    own_part(2)
-    prompt3(0)
-    own_part(3)
-    prompt1(3, far)
     between = {
-        (0, 0): lambda: prompt3(1),
+        (0, 0): lambda: (prompt3(1), prompt1(3, far)),
         (0, 2): lambda: prompt3(2),
         (1, 0): lambda: prompt3(3),
         (1, 2): lambda: reduce1(0),
@@ -512,8 +520,6 @@
     own_result(1)
     own_result(2)
     own_result(3)
-    for j in range(HEADS):
-        root_result(j)
 
     for j in range(HEADS):
         for i in range(3):
@@ -521,17 +527,20 @@
 
         @pl.when(core == 0)
         def _():
+            for i in range(4):
+                core_send(j, i).wait_send()
+
+        @pl.when(mesh_c0)
+        def _():
             for i in range(3):
                 p_send(j, i).wait_send()
-            for i in range(4):
-                core_send(j, i).wait_send()
 
         @pl.when(column)
         def _():
             for n in children(j):
                 z_send(j, n).wait_send()
 
-        if j > 0:
+        if j > 1:
             @pl.when(leaf & (z == 2))
             def _():
                 z_send(j, 4).wait_send()
@@ -559,6 +568,9 @@
 
         pltpu.make_async_copy(att_s.at[j], att_s.at[j], osem.at[0, j]).wait()
         pltpu.make_async_copy(dq_s.at[j], dq_s.at[j], osem.at[1, j]).wait()
+
+    for j in range(HEADS):
+        root_result(j)
 
 
 def main(mask, k, v, q, c):
@@ -606,7 +618,7 @@
             vmem((HEADS, NZ - 1) + block, BF16),
             vmem((HEADS,) + block, BF16),
             vmem((HEADS, 2, NY) + block, BF16),
-            dma((2, HEADS, 2)),
+            dma((5, HEADS, 2)),
             dma((2, HEADS)),
             dma((2, HEADS)),
             dma((HEADS, 3)),

time: 62.4 us -> 63.6 us (1.019)
  Pallas kernels: 61.4 us -> 62.6 us
    pallas_call x1, Pallas kernels: 58.9 us -> 60 us  [main(): pl.pallas_call(main_kernel, out_shape=(wide, wide, narrow, narrow), in_sp...]
where the time goes in v5:
time: 63.6 us; the launch traced here: 63.4 us
  Pallas kernels  62.6 us (98%)
  between operations  0.8 us (1%)
    pallas_call x1, Pallas kernels, main(): pl.pallas_call(main_kernel, out_shape=(wide, wide, narrow, narrow), in_sp...  60 us
    pallas_call x1, Pallas kernels, hand_on(): pl.pallas_call(hand_on_kernel, out_shape=[jax.ShapeDtypeStruct(a.shape, a...  2.52 us

profile of v5, /device:TPU:2, one launch (start us, length us, event | category | flops | bytes accessed | tf_op | source)
XLA Modules:
  0.0 63.4 jit_solution(2472711151190956706)
XLA Ops:
  0.6 60.0 %tree_attention.1 = (bf16[128,3584]{1,0:T(8,128)(2,1)}, bf16[128,3584]{1,0:T(8,128)(2,1)}, bf16[128,512]{1,0:T(8,128)(2,1)}, bf16[128,512]{1,0:T(8,128)(2,1)}) custom-call(s32[4,4]{1,0:T(4,128)} %mask_ref.1, bf16[128,512]{1,0:T(8,128)(2,1)} %k_ref.1, bf16[128,512]{1,0:T(8,128)(2,1)} %v_ref.1, bf16[128,3584]{1,0:T(8,128)(2,1)} %q_hbm.1, bf16[128,3584]{1,0:T(8,128)(2,1)} %c_hbm.1), custom_call_target="tpu_custom_call" | custom-call | tf_op jit(solution)/shard_map/tree_attention/pallas_call | solution.py:583
  60.7 2.5 %hand_on.1 = (bf16[128,3584]{1,0:T(8,128)(2,1)}, bf16[128,3584]{1,0:T(8,128)(2,1)}, bf16[128,512]{1,0:T(8,128)(2,1)}, bf16[128,512]{1,0:T(8,128)(2,1)}) custom-call(bf16[128,3584]{1,0:T(8,128)(2,1)} %get-tuple-element.8.refs_0_, bf16[128,3584]{1,0:T(8,128)(2,1)} %get-tuple-element.9.refs_1_, bf16[128,512]{1,0:T(8,128)(2,1)} %get-tuple-element.10.refs_2_, ...), custom_call_target="tpu_custom_call" | custom-call | tf_op jit(solution)/shard_map/hand_on/pallas_call | solution.py:675

commit v6 on v5

--- a/solution.py
+++ b/solution.py
@@ -41,6 +41,10 @@
 def partners(x, j):
     flip, mirror = x + 1 - 2 * (x % 2), 3 - x
     return (flip, mirror) if j % 2 == 0 else (mirror, flip)
+
+
+def drain(view, sem):
+    pltpu.make_async_copy(view, view, sem).wait()
 
 
 def others(x):
@@ -127,7 +131,7 @@
 
     def local(j, block, base):
         return [
-            pltpu.make_async_copy(ref.at[:, pl.ds(j * D, D)], kv.at[j, block, t], lsem.at[base, j, t])
+            pltpu.make_async_copy(ref.at[:, pl.ds(j * D, D)], kv.at[j, block, t], lsem.at[base])
             for t, ref in enumerate((k_ref, v_ref))
         ]
 
@@ -135,7 +139,7 @@
     def _():
         for j in range(HEADS):
             for b in range(QUARTERS):
-                for copy in local(j, b, 1 + b):
+                for copy in local(j, b, 1):
                     copy.start()
 
     for j in range(HEADS):
@@ -145,43 +149,35 @@
     def take_out(buf, hbm, i, j):
         for h in range(GROUP):
             cols, rows = pl.ds((j * GROUP + h) * D, D), pl.ds(h * D, D)
-            pltpu.make_async_copy(buf.at[j, rows], hbm.at[:, cols], osem.at[i, j]).start()
+            pltpu.make_async_copy(buf.at[j, rows], hbm.at[:, cols], osem.at[i]).start()
 
     hear_all(x, y, z, core)
 
     def y_send(j, n):
         blk = kv.at[j, x]
-        return remote(blk, blk, s_by.at[j, n - 1], r_t.at[j], device(x, n, 0, 0))
+        return remote(blk, blk, s_by.at[0], r_t.at[j], device(x, n, 0, 0))
 
     def z_send(j, n):
         blk = kv.at[j, x]
-        return remote(blk, blk, s_bz.at[j, n - 1], r_t.at[j], device(x, y, n, 0))
-
-    def children(j):
-        return (4, 5, 3, 6, 2, 7, 1) if j < 2 else (2, 6, 1, 7)
+        return remote(blk, blk, s_bz.at[0], r_t.at[j], device(x, y, n, 0))
 
     def pass_on(j):
-        for n in children(j):
+        for n in (2, 6, 1, 7):
             z_send(j, n).start()
 
     def x_send(j, base, ss, rs, i):
         pa, pb = partners(x, j)
         blk = kv.at[j, base + (x, x, pa)[i]]
-        return remote(blk, blk, ss.at[j, i], rs.at[j, i], device((pa, pb, pb)[i], y, z, core))
-
-    def x_arrival(j, base, ss, rs, i):
-        pa, pb = partners(x, j)
-        blk = kv.at[j, base + (pa, pb, opp)[i]]
-        remote(blk, blk, ss.at[j, i], rs.at[j, i], device((pa, pb, pb)[i], y, z, core)).wait_recv()
+        return remote(blk, blk, ss.at[0], rs.at[j, (0, 1, 1)[i]], device((pa, pb, pb)[i], y, z, core))
 
     def p_send(j, i):
         blk = kv.at[j, x]
-        return remote(blk, blk, s_pr.at[j, i], r_pr.at[j, i], device(others(x)[i], y, z, core))
+        return remote(blk, blk, s_pr.at[0], r_pr.at[j], device(others(x)[i], y, z, core))
 
     def core_send(j, i, base=0):
         n = x if i == 3 else others(x)[i]
         src, dst = kv.at[j, base + n], kv.at[j, n]
-        return remote(src, dst, s_c.at[j, i], r_c.at[j, i], device(x, y, z, 1 - core))
+        return remote(src, dst, s_c.at[0], r_c.at[j], device(x, y, z, 1 - core))
 
     def spread(j):
         for i in (2, 0, 1):
@@ -190,26 +186,23 @@
 
     @pl.when(is_root)
     def _():
+        drain(kv.at[:, pl.ds(0, 4)], lsem.at[1])
         for j in range(HEADS):
-            for b in range(QUARTERS):
-                for copy in local(j, b, 1 + b):
-                    copy.wait()
             for n in (2, 1, 3):
                 y_send(j, n).start()
             pass_on(j)
             core_send(j, 3).start()
 
+    drain(kv.at[:, pl.ds(4, 1)], lsem.at[0])
     for j in range(HEADS):
-        for copy in local(j, 4 + x, 0):
-            copy.wait()
         x_send(j, 4, s_own, r_own, 0).start()
         x_send(j, 4, s_own, r_own, 1).start()
 
     for j in range(HEADS):
         for h in range(GROUP):
             cols, rows = pl.ds((j * GROUP + h) * D, D), pl.ds(h * D, D)
-            pltpu.make_async_copy(q_hbm.at[:, cols], q_s.at[j, rows], qsem.at[0, j]).start()
-            pltpu.make_async_copy(c_hbm.at[:, cols], c_s.at[j, rows], qsem.at[1, j]).start()
+            pltpu.make_async_copy(q_hbm.at[:, cols], q_s.at[j, rows], qsem.at[0]).start()
+            pltpu.make_async_copy(c_hbm.at[:, cols], c_s.at[j, rows], qsem.at[1]).start()
 
     key = lax.broadcasted_iota(jnp.int32, (D, D), 0)
     query = lax.broadcasted_iota(jnp.int32, (D, D), 1)
@@ -230,22 +223,22 @@
             pass_on(j)
             spread(j)
 
-        x_arrival(j, 4, s_own, r_own, 0)
+        drain(kv.at[j, pl.ds(4, 1)], r_own.at[j, 0])
         x_send(j, 4, s_own, r_own, 2).start()
 
     def prompt1(j, here):
         @pl.when(here)
         def _():
             z_send(j, z).wait_recv()
-            if j > 1:
-                @pl.when(z == 2)
-                def _():
-                    z_send(j, 4).start()
-                    z_send(j, 3).start()
-
-                @pl.when(z == 6)
-                def _():
-                    z_send(j, 5).start()
+
+            @pl.when(z == 2)
+            def _():
+                z_send(j, 4).start()
+                z_send(j, 3).start()
+
+            @pl.when(z == 6)
+            def _():
+                z_send(j, 5).start()
 
             spread(j)
 
@@ -257,22 +250,20 @@
 
         @pl.when(mesh_c0)
         def _():
+            drain(kv.at[j, pl.ds(0, 3)], r_pr.at[j])
             for i in (0, 1, 2):
-                blk = kv.at[j, others(x)[i]]
-                remote(blk, blk, s_pr.at[j, i], r_pr.at[j, i], device(others(x)[i], y, z, core)).wait_recv()
                 core_send(j, i).start()
 
     def prompt_here(j):
         @pl.when(core == 1)
         def _():
-            for i in range(4):
-                core_send(j, i).wait_recv()
+            drain(kv.at[j, pl.ds(0, 4)], r_c.at[j])
 
     def own_part(j):
-        x_arrival(j, 4, s_own, r_own, 1)
-        x_arrival(j, 4, s_own, r_own, 2)
-        pltpu.make_async_copy(q_s.at[j], q_s.at[j], qsem.at[0, j]).wait()
-        pltpu.make_async_copy(c_s.at[j], c_s.at[j], qsem.at[1, j]).wait()
+        drain(kv.at[j, pl.ds(4, 2)], r_own.at[j, 1])
+        if j == 0:
+            drain(q_s, qsem.at[0])
+            drain(c_s, qsem.at[1])
         for at, width in TILES:
             cols = pl.ds(at, width)
             keys = kv[j, 4:8, 0].reshape(4 * D, D)
@@ -362,7 +353,7 @@
         take_out(dq_s, dq_hbm, 1, j)
 
     def hop(send, arrive, i, j, target):
-        return remote(send.at[j], arrive.at[j], ss.at[i, j], rs.at[i, j], target)
+        return remote(send.at[j], arrive.at[j], ss.at[i], rs.at[i, j], target)
 
     def own1(j):
         return hop(so1, ro1, 0, j, device(partners(x, j)[0], y, z, core))
@@ -374,13 +365,13 @@
         return hop(sc, rc, 2, j, device(x, y, z, 1 - core))
 
     def across(j, i):
-        return remote(sp1.at[j, i], rp1.at[j, i], s_a.at[j, i], r_a.at[j, i], device(others(x)[i], y, z, core))
+        return remote(sp1.at[j, i], rp1.at[j, i], s_a.at[0], r_a.at[j], device(others(x)[i], y, z, core))
 
     def to_column(j, n):
-        return remote(sz.at[j], rz.at[j, n - 1], s_z.at[j], r_z.at[j, n - 1], device(x, y, 0, core))
+        return remote(sz.at[j], rz.at[j, n - 1], s_z.at[0], r_z.at[j], device(x, y, 0, core))
 
     def to_root(j, t, n):
-        return remote(sy.at[j], ry.at[j, t, n], s_y.at[j], r_y.at[j, t, n], device(x, 0, 0, 0))
+        return remote(sy.at[j], ry.at[j, 4 * t + n - 1], s_y.at[0], r_y.at[j], device(x, 0, 0, 0))
 
     def reduce0(j):
         for b in range(QUARTERS):
@@ -409,8 +400,8 @@
 
     def reduce3(j):
         total = gs[j, x]
+        drain(rp1.at[j], r_a.at[j])
         for i in range(3):
-            across(j, i).wait_recv()
             total = total + rp1[j, i].astype(F32)
         part[j] = total
         sz[j] = total.astype(BF16)
@@ -423,8 +414,8 @@
         @pl.when(z == 0)
         def _():
             total = part[j]
+            drain(rz.at[j], r_z.at[j])
             for n in range(1, NZ):
-                to_column(j, n).wait_recv()
                 total = total + rz[j, n - 1].astype(F32)
             part[j] = total
             sy[j] = total.astype(BF16)
@@ -445,15 +436,14 @@
         @pl.when(is_root)
         def _():
             cols = pl.ds(j * D, D)
+            drain(ry.at[j], r_y.at[j])
             total = g[j, 4 + x, 0] + part[j]
             for n in range(1, NY):
-                to_root(j, 0, n).wait_recv()
-                total = total + ry[j, 0, n].astype(F32)
+                total = total + ry[j, n - 1].astype(F32)
             dk_ref[:, cols] = total.astype(BF16)
             total = g[j, 4 + x, 1]
             for n in range(NY):
-                to_root(j, 1, n).wait_recv()
-                total = total + ry[j, 1, n].astype(F32)
+                total = total + ry[j, 3 + n].astype(F32)
             dv_ref[:, cols] = total.astype(BF16)
 
     near = leaf & ((z < 3) | (z > 5))
@@ -462,20 +452,21 @@
     relay(1)
     prompt1(0, near)
     relay(2)
+    prompt1(1, near)
     relay(3)
+    prompt1(2, near)
+    own_part(0)
+    prompt1(3, near)
     prompt1(0, far)
-    prompt1(1, near)
-    own_part(0)
     own_part(1)
     prompt1(1, far)
     own_part(2)
-    prompt1(2, near)
+    prompt1(2, far)
+    own_part(3)
     prompt3(0)
-    own_part(3)
-    prompt1(2, far)
-    prompt1(3, near)
+    prompt1(3, far)
     between = {
-        (0, 0): lambda: (prompt3(1), prompt1(3, far)),
+        (0, 0): lambda: prompt3(1),
         (0, 2): lambda: prompt3(2),
         (1, 0): lambda: prompt3(3),
         (1, 2): lambda: reduce1(0),
@@ -521,53 +512,49 @@
     own_result(2)
     own_result(3)
 
-    for j in range(HEADS):
-        for i in range(3):
-            x_send(j, 4, s_own, r_own, i).wait_send()
-
-        @pl.when(core == 0)
-        def _():
-            for i in range(4):
-                core_send(j, i).wait_send()
-
-        @pl.when(mesh_c0)
-        def _():
-            for i in range(3):
-                p_send(j, i).wait_send()
-
-        @pl.when(column)
-        def _():
-            for n in children(j):
-                z_send(j, n).wait_send()
-
-        if j > 1:
-            @pl.when(leaf & (z == 2))
-            def _():
-                z_send(j, 4).wait_send()
-                z_send(j, 3).wait_send()
-
-            @pl.when(leaf & (z == 6))
-            def _():
-                z_send(j, 5).wait_send()
-
-        @pl.when(is_root)
-        def _():
-            for n in range(1, NY):
-                y_send(j, n).wait_send()
-
-        for copy in (own1(j), own2(j), pair(j), across(j, 0), across(j, 1), across(j, 2)):
-            copy.wait_send()
-
-        @pl.when(z != 0)
-        def _():
-            to_column(j, z).wait_send()
-
-        @pl.when((z == 0) & ((y != 0) | (core == 1)))
-        def _():
-            to_root(j, core, y).wait_send()
-
-        pltpu.make_async_copy(att_s.at[j], att_s.at[j], osem.at[0, j]).wait()
-        pltpu.make_async_copy(dq_s.at[j], dq_s.at[j], osem.at[1, j]).wait()
+    twelve = kv.at[pl.ds(0, 2), pl.ds(0, 6)]
+    sixteen = kv.at[pl.ds(0, 2)]
+    drain(twelve, s_own.at[0])
+
+    @pl.when(core == 0)
+    def _():
+        drain(sixteen, s_c.at[0])
+
+    @pl.when(mesh_c0)
+    def _():
+        drain(twelve, s_pr.at[0])
+
+    @pl.when(column)
+    def _():
+        drain(sixteen, s_bz.at[0])
+
+    @pl.when(leaf & (z == 2))
+    def _():
+        drain(kv.at[0], s_bz.at[0])
+
+    @pl.when(leaf & (z == 6))
+    def _():
+        drain(kv.at[0, pl.ds(0, 4)], s_bz.at[0])
+
+    @pl.when(is_root)
+    def _():
+        drain(twelve, s_by.at[0])
+
+    drain(so1, ss.at[0])
+    drain(so2, ss.at[1])
+    drain(sc, ss.at[2])
+    drain(sp1, s_a.at[0])
+
+    @pl.when(z != 0)
+    def _():
+        drain(sz, s_z.at[0])
+
+    @pl.when((z == 0) & ((y != 0) | (core == 1)))
+    def _():
+        drain(sy, s_y.at[0])
+
+    drain(att_s, osem.at[0])
+    drain(dq_s, osem.at[1])
 
     for j in range(HEADS):
         root_result(j)
@@ -617,27 +604,27 @@
             vmem((HEADS,) + block, BF16),
             vmem((HEADS, NZ - 1) + block, BF16),
             vmem((HEADS,) + block, BF16),
-            vmem((HEADS, 2, NY) + block, BF16),
-            dma((5, HEADS, 2)),
-            dma((2, HEADS)),
-            dma((2, HEADS)),
-            dma((HEADS, 3)),
-            dma((HEADS, 3)),
-            dma((HEADS, 3)),
-            dma((HEADS, 3)),
-            dma((HEADS, NY - 1)),
-            dma((HEADS, NZ - 1)),
+            vmem((HEADS, 2 * NY - 1) + block, BF16),
+            dma((2,)),
+            dma((2,)),
+            dma((2,)),
+            dma((1,)),
+            dma((HEADS, 2)),
+            dma((1,)),
             dma((HEADS,)),
-            dma((HEADS, 4)),
-            dma((HEADS, 4)),
+            dma((1,)),
+            dma((1,)),
+            dma((HEADS,)),
+            dma((1,)),
+            dma((HEADS,)),
+            dma((3,)),
             dma((3, HEADS)),
-            dma((3, HEADS)),
-            dma((HEADS, 3)),
-            dma((HEADS, 3)),
+            dma((1,)),
             dma((HEADS,)),
-            dma((HEADS, 2, NY)),
+            dma((1,)),
             dma((HEADS,)),
-            dma((HEADS, NZ - 1)),
+            dma((1,)),
+            dma((HEADS,)),
         ],
         compiler_params=pltpu.CompilerParams(
             collective_id=0, has_side_effects=True, vmem_limit_bytes=60 * 2**20

time: 63.6 us -> 60.3 us (0.948)
  Pallas kernels: 62.6 us -> 59.3 us
    pallas_call x1, Pallas kernels: 60 us -> 56.8 us  [main(): pl.pallas_call(main_kernel, out_shape=(wide, wide, narrow, narrow), in_sp...]
where the time goes in v6:
time: 60.3 us; the launch traced here: 60.1 us
  Pallas kernels  59.3 us (98%)
  between operations  0.8 us (1%)
    pallas_call x1, Pallas kernels, main(): pl.pallas_call(main_kernel, out_shape=(wide, wide, narrow, narrow), in_sp...  56.8 us
    pallas_call x1, Pallas kernels, hand_on(): pl.pallas_call(hand_on_kernel, out_shape=[jax.ShapeDtypeStruct(a.shape, a...  2.52 us

profile of v6, /device:TPU:2, one launch (start us, length us, event | category | flops | bytes accessed | tf_op | source)
XLA Modules:
  0.0 60.1 jit_solution(6997902837838365632)
XLA Ops:
  0.6 56.8 %tree_attention.1 = (bf16[128,3584]{1,0:T(8,128)(2,1)}, bf16[128,3584]{1,0:T(8,128)(2,1)}, bf16[128,512]{1,0:T(8,128)(2,1)}, bf16[128,512]{1,0:T(8,128)(2,1)}) custom-call(s32[4,4]{1,0:T(4,128)} %mask_ref.1, bf16[128,512]{1,0:T(8,128)(2,1)} %k_ref.1, bf16[128,512]{1,0:T(8,128)(2,1)} %v_ref.1, bf16[128,3584]{1,0:T(8,128)(2,1)} %q_hbm.1, bf16[128,3584]{1,0:T(8,128)(2,1)} %c_hbm.1), custom_call_target="tpu_custom_call" | custom-call | tf_op jit(solution)/shard_map/tree_attention/pallas_call | solution.py:570
  57.4 2.5 %hand_on.1 = (bf16[128,3584]{1,0:T(8,128)(2,1)}, bf16[128,3584]{1,0:T(8,128)(2,1)}, bf16[128,512]{1,0:T(8,128)(2,1)}, bf16[128,512]{1,0:T(8,128)(2,1)}) custom-call(bf16[128,3584]{1,0:T(8,128)(2,1)} %get-tuple-element.8.refs_0_, bf16[128,3584]{1,0:T(8,128)(2,1)} %get-tuple-element.9.refs_1_, bf16[128,512]{1,0:T(8,128)(2,1)} %get-tuple-element.10.refs_2_, ...), custom_call_target="tpu_custom_call" | custom-call | tf_op jit(solution)/shard_map/hand_on/pallas_call | solution.py:662

commit v7 on v6

--- a/solution.py
+++ b/solution.py
@@ -113,7 +113,7 @@
 def main_kernel(
     mask_ref, k_ref, v_ref, q_hbm, c_hbm,
     att_hbm, dq_hbm, dk_ref, dv_ref,
-    kv, q_s, c_s, att_s, dq_s, bias, po, dpo, mo, lo, fo, de, sp, dpp, ps, dss, vt,
+    kv, q_s, c_s, att_s, dq_s, bias, po, dpo, mo, lo, fo, de, sp, dpp, pb, oo, ps, dss, vt,
     g, so1, ro1, so2, ro2, sc, rc, gs, sp1, rp1, part, sz, rz, sy, ry,
     lsem, qsem, osem, s_own, r_own, s_pr, r_pr, s_by, s_bz, r_t, s_c, r_c,
     ss, rs, s_a, r_a, s_y, r_y, s_z, r_z,
@@ -221,13 +221,15 @@
         def _():
             y_send(j, y).wait_recv()
             pass_on(j)
-            spread(j)
 
         drain(kv.at[j, pl.ds(4, 1)], r_own.at[j, 0])
         x_send(j, 4, s_own, r_own, 2).start()
 
-    def prompt1(j, here):
-        @pl.when(here)
+    relaying = leaf & ((z == 2) | (z == 6))
+    quiet = leaf & (z != 2) & (z != 6)
+
+    def forward(j):
+        @pl.when(relaying)
         def _():
             z_send(j, z).wait_recv()
 
@@ -240,6 +242,13 @@
             def _():
                 z_send(j, 5).start()
 
+    def prompt1(j):
+        @pl.when(quiet)
+        def _():
+            z_send(j, z).wait_recv()
+
+        @pl.when(mesh_c0)
+        def _():
             spread(j)
 
     def prompt3(j):
@@ -264,8 +273,10 @@
         if j == 0:
             drain(q_s, qsem.at[0])
             drain(c_s, qsem.at[1])
+        for b in range(QUARTERS):
+            vt[:, pl.ds(b * D, D)] = kv[j, 4 + b, 1].T
         for at, width in TILES:
-            cols = pl.ds(at, width)
+            cols, wide = pl.ds(at, width), pl.ds(0, width)
             keys = kv[j, 4:8, 0].reshape(4 * D, D)
             values = kv[j, 4:8, 1].reshape(4 * D, D)
             po[j, :, cols] = nt(keys, q_s[j, cols, :]) + bias[:, pl.ds(0, width)]
@@ -278,14 +289,16 @@
             for b in range(QUARTERS):
                 p = jnp.exp2((po[j, pl.ds(b * D, D), cols] - top) * EXP_SCALE)
                 po[j, pl.ds(b * D, D), cols] = p
+                pb[pl.ds(b * D, D), wide] = p.astype(BF16)
                 part_sum = fold_sum(p)
                 total = part_sum if total is None else total + part_sum
             mo[j, :, cols] = top
             lo[j, :, cols] = jnp.sum(total, axis=0, keepdims=True)
+            oo[j, :, cols] = nn(vt[:, pl.ds(0, 4 * D)], pb[:, wide])
             dpo[j, :, cols] = nt(values, c_s[j, cols, :])
 
     def flip_values(j):
-        for b in range(2 * QUARTERS):
+        for b in range(QUARTERS):
             vt[:, pl.ds(b * D, D)] = kv[j, b, 1].T
 
     def prompt_part(j, at, width):
@@ -314,8 +327,8 @@
         for b in range(QUARTERS):
             rows = pl.ds(b * D, D)
             ps[j, rows, cols] = (sp[rows, wide] * inverse).astype(BF16)
-            ps[j, pl.ds((4 + b) * D, D), cols] = (po[j, rows, cols] * shrink).astype(BF16)
-        out_t = nn(vt[...], ps[j, :, cols]).astype(BF16)
+        out_t = nn(vt[:, pl.ds(0, 4 * D)], ps[j, pl.ds(0, 4 * D), cols])
+        out_t = (out_t + oo[j, :, cols] * shrink).astype(BF16)
         deltas = []
         for i in range(width // D):
             lanes, rows = slice(i * D, i * D + D), pl.ds(at + i * D, D)
@@ -333,8 +346,10 @@
             cols = pl.ds(at, width)
             for b in range(QUARTERS):
                 rows = pl.ds(b * D, D)
+                p = po[j, rows, cols] * fo[j, :, cols]
+                ps[j, pl.ds((4 + b) * D, D), cols] = p.astype(BF16)
                 dss[j, pl.ds((4 + b) * D, D), cols] = (
-                    (po[j, rows, cols] * fo[j, :, cols]) * (dpo[j, rows, cols] - de[j, :, cols])
+                    p * (dpo[j, rows, cols] - de[j, :, cols])
                 ).astype(BF16)
         key_terms(j, 4)
 
@@ -446,25 +461,23 @@
                 total = total + ry[j, 3 + n].astype(F32)
             dv_ref[:, cols] = total.astype(BF16)
 
-    near = leaf & ((z < 3) | (z > 5))
-    far = leaf & (z > 2) & (z < 6)
     relay(0)
     relay(1)
-    prompt1(0, near)
+    forward(0)
     relay(2)
-    prompt1(1, near)
+    forward(1)
     relay(3)
-    prompt1(2, near)
+    forward(2)
     own_part(0)
-    prompt1(3, near)
-    prompt1(0, far)
+    prompt1(0)
+    forward(3)
     own_part(1)
-    prompt1(1, far)
+    prompt1(1)
     own_part(2)
-    prompt1(2, far)
+    prompt1(2)
+    prompt3(0)
     own_part(3)
-    prompt3(0)
-    prompt1(3, far)
+    prompt1(3)
     between = {
         (0, 0): lambda: prompt3(1),
         (0, 2): lambda: prompt3(2),
@@ -487,9 +500,9 @@
     own_terms(0)
     reduce1(3)
     own_reduce1(0)
-    reduce3(2)
     own_terms(1)
     own_reduce1(1)
+    reduce3(2)
     own_terms(2)
     own_reduce1(2)
     reduce4(0)
@@ -587,6 +600,8 @@
             vmem((HEADS, 1, WIDE), F32),
             vmem((4 * D, 2 * D), F32),
             vmem((4 * D, 2 * D), F32),
+            vmem((4 * D, 2 * D), BF16),
+            vmem((HEADS, D, WIDE), F32),
             vmem((HEADS, 8 * D, WIDE), BF16),
             vmem((HEADS, 8 * D, WIDE), BF16),
             vmem((D, 8 * D), BF16),

time: 60.3 us -> 59.9 us (level)
  no operation moved by 1% of the time
where the time goes in v7:
time: 59.9 us; the launch traced here: 59.7 us
  Pallas kernels  58.9 us (98%)
  between operations  0.8 us (1%)
    pallas_call x1, Pallas kernels, main(): pl.pallas_call(main_kernel, out_shape=(wide, wide, narrow, narrow), in_sp...  56.4 us
    pallas_call x1, Pallas kernels, hand_on(): pl.pallas_call(hand_on_kernel, out_shape=[jax.ShapeDtypeStruct(a.shape, a...  2.52 us

profile of v7, /device:TPU:2, one launch (start us, length us, event | category | flops | bytes accessed | tf_op | source)
XLA Modules:
  0.0 59.7 jit_solution(5210666986475529037)
XLA Ops:
  0.6 56.4 %tree_attention.1 = (bf16[128,3584]{1,0:T(8,128)(2,1)}, bf16[128,3584]{1,0:T(8,128)(2,1)}, bf16[128,512]{1,0:T(8,128)(2,1)}, bf16[128,512]{1,0:T(8,128)(2,1)}) custom-call(s32[4,4]{1,0:T(4,128)} %mask_ref.1, bf16[128,512]{1,0:T(8,128)(2,1)} %k_ref.1, bf16[128,512]{1,0:T(8,128)(2,1)} %v_ref.1, bf16[128,3584]{1,0:T(8,128)(2,1)} %q_hbm.1, bf16[128,3584]{1,0:T(8,128)(2,1)} %c_hbm.1), custom_call_target="tpu_custom_call" | custom-call | tf_op jit(solution)/shard_map/tree_attention/pallas_call | solution.py:583
  57.0 2.5 %hand_on.1 = (bf16[128,3584]{1,0:T(8,128)(2,1)}, bf16[128,3584]{1,0:T(8,128)(2,1)}, bf16[128,512]{1,0:T(8,128)(2,1)}, bf16[128,512]{1,0:T(8,128)(2,1)}) custom-call(bf16[128,3584]{1,0:T(8,128)(2,1)} %get-tuple-element.8.refs_0_, bf16[128,3584]{1,0:T(8,128)(2,1)} %get-tuple-element.9.refs_1_, bf16[128,512]{1,0:T(8,128)(2,1)} %get-tuple-element.10.refs_2_, ...), custom_call_target="tpu_custom_call" | custom-call | tf_op jit(solution)/shard_map/hand_on/pallas_call | solution.py:677

commit v8 on v7

--- a/solution.py
+++ b/solution.py
@@ -159,10 +159,10 @@
 
     def z_send(j, n):
         blk = kv.at[j, x]
-        return remote(blk, blk, s_bz.at[0], r_t.at[j], device(x, y, n, 0))
+        return remote(blk, blk, s_bz.at[1 if j == 0 else 0], r_t.at[j], device(x, y, n, 0))
 
     def pass_on(j):
-        for n in (2, 6, 1, 7):
+        for n in (4, 5, 3, 6, 2, 7, 1) if j == 0 else (2, 6, 1, 7):
             z_send(j, n).start()
 
     def x_send(j, base, ss, rs, i):
@@ -172,7 +172,7 @@
 
     def p_send(j, i):
         blk = kv.at[j, x]
-        return remote(blk, blk, s_pr.at[0], r_pr.at[j], device(others(x)[i], y, z, core))
+        return remote(blk, blk, s_pr.at[0], r_pr.at[j, i], device(others(x)[i], y, z, core))
 
     def core_send(j, i, base=0):
         n = x if i == 3 else others(x)[i]
@@ -242,12 +242,16 @@
             def _():
                 z_send(j, 5).start()
 
-    def prompt1(j):
-        @pl.when(quiet)
+    far = (z > 2) & (z < 6)
+
+    def prompt1(j, here=None):
+        here = mesh_c0 if here is None else mesh_c0 & here
+
+        @pl.when(here & (leaf if j == 0 else quiet))
         def _():
             z_send(j, z).wait_recv()
 
-        @pl.when(mesh_c0)
+        @pl.when(here)
         def _():
             spread(j)
 
@@ -259,8 +263,8 @@
 
         @pl.when(mesh_c0)
         def _():
-            drain(kv.at[j, pl.ds(0, 3)], r_pr.at[j])
             for i in (0, 1, 2):
+                drain(kv.at[j, pl.ds(0, 1)], r_pr.at[j, i])
                 core_send(j, i).start()
 
     def prompt_here(j):
@@ -463,19 +467,19 @@
 
     relay(0)
     relay(1)
-    forward(0)
     relay(2)
+    relay(3)
+    prompt1(0, ~far)
     forward(1)
-    relay(3)
+    own_part(0)
+    prompt1(0, far)
     forward(2)
-    own_part(0)
-    prompt1(0)
+    own_part(1)
     forward(3)
-    own_part(1)
     prompt1(1)
     own_part(2)
+    prompt3(0)
     prompt1(2)
-    prompt3(0)
     own_part(3)
     prompt1(3)
     between = {
@@ -516,10 +520,10 @@
     reduce4(2)
     query_part(1)
     own_reduce2(2)
+    reduce4(3)
+    own_reduce2(3)
     query_part(2)
     query_part(3)
-    reduce4(3)
-    own_reduce2(3)
     own_result(0)
     own_result(1)
     own_result(2)
@@ -539,15 +543,16 @@
 
     @pl.when(column)
     def _():
-        drain(sixteen, s_bz.at[0])
+        drain(twelve, s_bz.at[0])
+        drain(kv.at[0, pl.ds(0, 7)], s_bz.at[1])
 
     @pl.when(leaf & (z == 2))
     def _():
-        drain(kv.at[0], s_bz.at[0])
+        drain(kv.at[0, pl.ds(0, 6)], s_bz.at[0])
 
     @pl.when(leaf & (z == 6))
     def _():
-        drain(kv.at[0, pl.ds(0, 4)], s_bz.at[0])
+        drain(kv.at[0, pl.ds(0, 3)], s_bz.at[0])
 
     @pl.when(is_root)
     def _():
@@ -626,9 +631,9 @@
             dma((1,)),
             dma((HEADS, 2)),
             dma((1,)),
-            dma((HEADS,)),
+            dma((HEADS, 3)),
             dma((1,)),
-            dma((1,)),
+            dma((2,)),
             dma((HEADS,)),
             dma((1,)),
             dma((HEADS,)),

time: 59.9 us -> 58.9 us (0.983)
  Pallas kernels: 58.9 us -> 57.9 us
    pallas_call x1, Pallas kernels: 56.4 us -> 55.3 us  [main(): pl.pallas_call(main_kernel, out_shape=(wide, wide, narrow, narrow), in_sp...]
where the time goes in v8:
time: 58.9 us; the launch traced here: 58.7 us
  Pallas kernels  57.9 us (98%)
  between operations  0.8 us (1%)
    pallas_call x1, Pallas kernels, main(): pl.pallas_call(main_kernel, out_shape=(wide, wide, narrow, narrow), in_sp...  55.3 us
    pallas_call x1, Pallas kernels, hand_on(): pl.pallas_call(hand_on_kernel, out_shape=[jax.ShapeDtypeStruct(a.shape, a...  2.52 us

profile of v8, /device:TPU:2, one launch (start us, length us, event | category | flops | bytes accessed | tf_op | source)
XLA Modules:
  0.0 58.7 jit_solution(4671314773206631635)
XLA Ops:
  0.6 55.3 %tree_attention.1 = (bf16[128,3584]{1,0:T(8,128)(2,1)}, bf16[128,3584]{1,0:T(8,128)(2,1)}, bf16[128,512]{1,0:T(8,128)(2,1)}, bf16[128,512]{1,0:T(8,128)(2,1)}) custom-call(s32[4,4]{1,0:T(4,128)} %mask_ref.1, bf16[128,512]{1,0:T(8,128)(2,1)} %k_ref.1, bf16[128,512]{1,0:T(8,128)(2,1)} %v_ref.1, bf16[128,3584]{1,0:T(8,128)(2,1)} %q_hbm.1, bf16[128,3584]{1,0:T(8,128)(2,1)} %c_hbm.1), custom_call_target="tpu_custom_call" | custom-call | tf_op jit(solution)/shard_map/tree_attention/pallas_call | solution.py:588
  56.0 2.5 %hand_on.1 = (bf16[128,3584]{1,0:T(8,128)(2,1)}, bf16[128,3584]{1,0:T(8,128)(2,1)}, bf16[128,512]{1,0:T(8,128)(2,1)}, bf16[128,512]{1,0:T(8,128)(2,1)}) custom-call(bf16[128,3584]{1,0:T(8,128)(2,1)} %get-tuple-element.8.refs_0_, bf16[128,3584]{1,0:T(8,128)(2,1)} %get-tuple-element.9.refs_1_, bf16[128,512]{1,0:T(8,128)(2,1)} %get-tuple-element.10.refs_2_, ...), custom_call_target="tpu_custom_call" | custom-call | tf_op jit(solution)/shard_map/hand_on/pallas_call | solution.py:682

commit v9 on v8

--- a/solution.py
+++ b/solution.py
@@ -113,7 +113,7 @@
 def main_kernel(
     mask_ref, k_ref, v_ref, q_hbm, c_hbm,
     att_hbm, dq_hbm, dk_ref, dv_ref,
-    kv, q_s, c_s, att_s, dq_s, bias, po, dpo, mo, lo, fo, de, sp, dpp, pb, oo, ps, dss, vt,
+    kv, q_s, c_s, att_s, dq_s, bias, po, mo, lo, fo, de, sp, dpp, pb, oo, ps, dss, vt,
     g, so1, ro1, so2, ro2, sc, rc, gs, sp1, rp1, part, sz, rz, sy, ry,
     lsem, qsem, osem, s_own, r_own, s_pr, r_pr, s_by, s_bz, r_t, s_c, r_c,
     ss, rs, s_a, r_a, s_y, r_y, s_z, r_z,
@@ -282,7 +282,6 @@
         for at, width in TILES:
             cols, wide = pl.ds(at, width), pl.ds(0, width)
             keys = kv[j, 4:8, 0].reshape(4 * D, D)
-            values = kv[j, 4:8, 1].reshape(4 * D, D)
             po[j, :, cols] = nt(keys, q_s[j, cols, :]) + bias[:, pl.ds(0, width)]
             top = None
             for b in range(QUARTERS):
@@ -299,7 +298,6 @@
             mo[j, :, cols] = top
             lo[j, :, cols] = jnp.sum(total, axis=0, keepdims=True)
             oo[j, :, cols] = nn(vt[:, pl.ds(0, 4 * D)], pb[:, wide])
-            dpo[j, :, cols] = nt(values, c_s[j, cols, :])
 
     def flip_values(j):
         for b in range(QUARTERS):
@@ -347,13 +345,14 @@
 
     def own_terms(j):
         for at, width in TILES:
-            cols = pl.ds(at, width)
+            cols, wide = pl.ds(at, width), pl.ds(0, width)
+            dpp[:, wide] = nt(kv[j, 4:8, 1].reshape(4 * D, D), c_s[j, cols, :])
             for b in range(QUARTERS):
                 rows = pl.ds(b * D, D)
                 p = po[j, rows, cols] * fo[j, :, cols]
                 ps[j, pl.ds((4 + b) * D, D), cols] = p.astype(BF16)
                 dss[j, pl.ds((4 + b) * D, D), cols] = (
-                    p * (dpo[j, rows, cols] - de[j, :, cols])
+                    p * (dpp[rows, wide] - de[j, :, cols])
                 ).astype(BF16)
         key_terms(j, 4)
 
@@ -598,7 +597,6 @@
             vmem((HEADS, WIDE, D), BF16),
             vmem((4 * D, 2 * D), F32),
             vmem((HEADS, 4 * D, WIDE), F32),
-            vmem((HEADS, 4 * D, WIDE), F32),
             vmem((HEADS, 1, WIDE), F32),
             vmem((HEADS, 1, WIDE), F32),
             vmem((HEADS, 1, WIDE), F32),

time: 58.9 us -> 59.3 us (level)
  no operation moved by 1% of the time
where the time goes in v9:
time: 59.3 us; the launch traced here: 59.1 us
  Pallas kernels  58.3 us (98%)
  between operations  0.8 us (1%)
    pallas_call x1, Pallas kernels, main(): pl.pallas_call(main_kernel, out_shape=(wide, wide, narrow, narrow), in_sp...  55.8 us
    pallas_call x1, Pallas kernels, hand_on(): pl.pallas_call(hand_on_kernel, out_shape=[jax.ShapeDtypeStruct(a.shape, a...  2.52 us

profile of v9, /device:TPU:2, one launch (start us, length us, event | category | flops | bytes accessed | tf_op | source)
XLA Modules:
  0.0 59.1 jit_solution(6215241335157978826)
XLA Ops:
  0.6 55.8 %tree_attention.1 = (bf16[128,3584]{1,0:T(8,128)(2,1)}, bf16[128,3584]{1,0:T(8,128)(2,1)}, bf16[128,512]{1,0:T(8,128)(2,1)}, bf16[128,512]{1,0:T(8,128)(2,1)}) custom-call(s32[4,4]{1,0:T(4,128)} %mask_ref.1, bf16[128,512]{1,0:T(8,128)(2,1)} %k_ref.1, bf16[128,512]{1,0:T(8,128)(2,1)} %v_ref.1, bf16[128,3584]{1,0:T(8,128)(2,1)} %q_hbm.1, bf16[128,3584]{1,0:T(8,128)(2,1)} %c_hbm.1), custom_call_target="tpu_custom_call" | custom-call | tf_op jit(solution)/shard_map/tree_attention/pallas_call | solution.py:587
  56.4 2.5 %hand_on.1 = (bf16[128,3584]{1,0:T(8,128)(2,1)}, bf16[128,3584]{1,0:T(8,128)(2,1)}, bf16[128,512]{1,0:T(8,128)(2,1)}, bf16[128,512]{1,0:T(8,128)(2,1)}) custom-call(bf16[128,3584]{1,0:T(8,128)(2,1)} %get-tuple-element.8.refs_0_, bf16[128,3584]{1,0:T(8,128)(2,1)} %get-tuple-element.9.refs_1_, bf16[128,512]{1,0:T(8,128)(2,1)} %get-tuple-element.10.refs_2_, ...), custom_call_target="tpu_custom_call" | custom-call | tf_op jit(solution)/shard_map/hand_on/pallas_call | solution.py:680

commit v10 on v8

--- a/solution.py
+++ b/solution.py
@@ -513,17 +513,17 @@
     own_terms(3)
     reduce3(3)
     own_reduce1(3)
+    query_part(0)
+    query_part(1)
+    query_part(2)
+    query_part(3)
     own_reduce2(0)
     reduce4(1)
-    query_part(0)
     own_reduce2(1)
     reduce4(2)
-    query_part(1)
     own_reduce2(2)
     reduce4(3)
     own_reduce2(3)
-    query_part(2)
-    query_part(3)
     own_result(0)
     own_result(1)
     own_result(2)

time: 58.9 us -> 58.9 us (level)
  no operation moved by 1% of the time
where the time goes in v10:
time: 58.9 us; the launch traced here: 58.7 us
  Pallas kernels  57.9 us (98%)
  between operations  0.8 us (1%)
    pallas_call x1, Pallas kernels, main(): pl.pallas_call(main_kernel, out_shape=(wide, wide, narrow, narrow), in_sp...  55.3 us
    pallas_call x1, Pallas kernels, hand_on(): pl.pallas_call(hand_on_kernel, out_shape=[jax.ShapeDtypeStruct(a.shape, a...  2.52 us

profile of v10, /device:TPU:2, one launch (start us, length us, event | category | flops | bytes accessed | tf_op | source)
XLA Modules:
  0.0 58.7 jit_solution(11015172908524927707)
XLA Ops:
  0.6 55.3 %tree_attention.1 = (bf16[128,3584]{1,0:T(8,128)(2,1)}, bf16[128,3584]{1,0:T(8,128)(2,1)}, bf16[128,512]{1,0:T(8,128)(2,1)}, bf16[128,512]{1,0:T(8,128)(2,1)}) custom-call(s32[4,4]{1,0:T(4,128)} %mask_ref.1, bf16[128,512]{1,0:T(8,128)(2,1)} %k_ref.1, bf16[128,512]{1,0:T(8,128)(2,1)} %v_ref.1, bf16[128,3584]{1,0:T(8,128)(2,1)} %q_hbm.1, bf16[128,3584]{1,0:T(8,128)(2,1)} %c_hbm.1), custom_call_target="tpu_custom_call" | custom-call | tf_op jit(solution)/shard_map/tree_attention/pallas_call | solution.py:588
  56.0 2.5 %hand_on.1 = (bf16[128,3584]{1,0:T(8,128)(2,1)}, bf16[128,3584]{1,0:T(8,128)(2,1)}, bf16[128,512]{1,0:T(8,128)(2,1)}, bf16[128,512]{1,0:T(8,128)(2,1)}) custom-call(bf16[128,3584]{1,0:T(8,128)(2,1)} %get-tuple-element.8.refs_0_, bf16[128,3584]{1,0:T(8,128)(2,1)} %get-tuple-element.9.refs_1_, bf16[128,512]{1,0:T(8,128)(2,1)} %get-tuple-element.10.refs_2_, ...), custom_call_target="tpu_custom_call" | custom-call | tf_op jit(solution)/shard_map/hand_on/pallas_call | solution.py:682
